TPU v7x, 256 devices: a whole 4x4x8 slice. The times are simulated.
256 devices in a mesh: grp: 4 (over x_lo, core), row: 4 (over y), col: 16 (over z, x_hi).
Axes of the slice: x: 4 (x_hi: 2, x_lo: 2; x = x_hi * 2 + x_lo), y: 4, z: 8, core: 2. Of those that a mesh axis runs over, the one named last changes fastest.
Arguments:
- block_rows: bfloat16 [8, 304, 10240], P('grp', None, ('row', 'col')), may hold values from -6 to 6
- inverse_factor: float32 [8, 304, 304], P('grp'), as said below
- live_rows: int32 [8], P('grp'), may hold values from 50 to 304, as said below
- shift: float32 [10240], P(('grp', 'row', 'col')), may hold values from 0.5 to 2
Outputs:
- factored: float32 [10240, 10240], P(('grp', 'row'), 'col')
Inputs may be any that keep to these rules, and one draw needn't show every extreme that they name: `live_rows`: every block uses between 50 and 304 rows; some block uses exactly 304 and some exactly 50. `inverse_factor`: each block's matrix is lower triangular with a positive diagonal.
All inputs are finite; a program needn't handle non-finite values.
Results may differ from a plain program's by a relative error of at most 0.0043.
Values may be sent and summed in bfloat16 or wider, within the bound.
A program may use at most 128 MiB of HBM per device.

v0:
```python
import jax
import jax.numpy as jnp
from jax import lax
from jax.sharding import PartitionSpec as P

PW = 1024
PANELS = 1
NPAN = 10


def local(block_rows, inverse_factor, live_rows, shift):
    highest = lax.Precision.HIGHEST
    groups = lax.axis_size("grp")
    rowcount = lax.axis_size("row")
    colcount = lax.axis_size("col")
    owners = groups * rowcount
    slab = PW // owners
    window = slab // colcount
    group_index = lax.axis_index("grp")
    row_index = lax.axis_index("row")
    col_index = lax.axis_index("col")
    blocks, padded, local_cols = block_rows.shape
    stacked_rows = blocks * padded
    local_rows = NPAN * slab
    ordinal = jnp.arange(padded, dtype=jnp.int32)
    live_mask = (ordinal[None, :] < live_rows[:, None]).astype(jnp.float32)
    masked_factor = inverse_factor * live_mask[:, :, None] * live_mask[:, None, :]
    whitened = jnp.einsum(
        "bij,bjm->mbi", masked_factor, block_rows.astype(jnp.float32), precision=highest
    )
    whitened = whitened.astype(jnp.bfloat16).reshape(groups, NPAN, window, stacked_rows)
    turned = jnp.transpose(whitened, (1, 0, 2, 3)).reshape(NPAN, groups, 1, window, stacked_rows)
    col_side = lax.all_gather(turned, "row", axis=2, tiled=True).reshape(
        NPAN * owners * window, stacked_rows
    )
    row_side = lax.all_gather(whitened, "col", axis=2, tiled=True).reshape(
        groups * local_rows, stacked_rows
    )
    schur_tile = lax.psum_scatter(
        lax.dot_general(
            row_side, col_side, (((1,), (1,)), ((), ())), preferred_element_type=jnp.float32
        ),
        "grp",
        scatter_dimension=0,
        tiled=True,
    )
    panel_ids = jnp.arange(NPAN, dtype=jnp.int32)
    slab_ids = jnp.arange(slab, dtype=jnp.int32)
    owner_ids = jnp.arange(owners, dtype=jnp.int32)
    window_ids = jnp.arange(window, dtype=jnp.int32)
    own_owner = group_index * rowcount + row_index
    row_global = ((panel_ids[:, None] * owners + own_owner) * slab + slab_ids[None, :]).reshape(-1)
    col_global = (
        (panel_ids[:, None, None] * owners + owner_ids[None, :, None]) * slab
        + col_index * window
        + window_ids[None, None, :]
    ).reshape(-1)
    shift_grid = shift.reshape(NPAN, 1, window)
    col_shift = jnp.where(owner_ids[None, :, None] == own_owner, shift_grid, 0.0).reshape(-1)
    schur_tile = schur_tile + jnp.where(
        row_global[:, None] == col_global[None, :], col_shift[None, :], 0.0
    )
    grid_view = schur_tile.reshape(local_rows, NPAN, owners, window)
    own_panel = jnp.transpose(grid_view[:, 0], (1, 2, 0))
    panel_cols_t = lax.all_gather(own_panel, "col", axis=1, tiled=True).reshape(PW, local_rows)
    own_piece = panel_cols_t[:, 0:slab].T
    diagonal_block = lax.all_gather(own_piece, ("grp", "row"), axis=0, tiled=True)
    cholesky_factor = jnp.linalg.cholesky(diagonal_block)
    row_factor_t = jax.scipy.linalg.solve_triangular(cholesky_factor, panel_cols_t, lower=True)
    row_factor = row_factor_t.T
    own_rows = schur_tile.reshape(NPAN, slab, -1)[0]
    gathered_rows = lax.all_gather(own_rows, ("grp", "row"), axis=0, tiled=True)
    col_factor = jax.scipy.linalg.solve_triangular(cholesky_factor, gathered_rows, lower=True).T
    panel_piece = lax.dynamic_slice_in_dim(
        row_factor_t.reshape(owners, slab, local_rows), col_index * window, window, 1
    )
    panel_piece = panel_piece.reshape(owners * window, local_rows).T
    panel_cols_global = col_global.reshape(NPAN, -1)[0]
    finished = [
        jnp.where(row_global[:, None] >= panel_cols_global[None, :], panel_piece, 0.0).reshape(
            local_rows, 1, -1
        )
    ]
    boundary = PW
    row_kept = jnp.where(row_global[:, None] >= boundary, row_factor, 0.0)
    col_kept = jnp.where(col_global[:, None] >= boundary, col_factor, 0.0)
    schur_tile = schur_tile - jnp.dot(
        row_kept, col_kept.T, precision=highest, preferred_element_type=jnp.float32
    )
    trailing = schur_tile.reshape(local_rows, NPAN, -1)[:, PANELS:]
    trailing = jnp.where(row_global[:, None, None] >= PANELS * PW, trailing, 0.0)
    return jnp.concatenate(finished + [trailing], axis=1).reshape(local_rows, -1)


def solution(mesh):
    in_specs = (
        P("grp", None, ("row", "col")),
        P("grp", None, None),
        P("grp"),
        P(("grp", "row", "col")),
    )
    out_specs = P(("grp", "row"), "col")
    return jax.shard_map(local, mesh=mesh, in_specs=in_specs, out_specs=out_specs, check_vma=False)
```

profile of v0, /device:TPU:1, one launch (start us, length us, event | category | flops | bytes accessed | tf_op | source)
XLA Modules:
  0.0 720.3 jit_solution(5468625018093180597)
XLA Ops:
  11.0 13.4 %all-gather = bf16[10,4,16,608]{3,1,0,2:T(4,128)(2,1)S(1)} all-gather(bf16[10,4,4,608]{3,1,0,2:T(4,128)(2,1)S(1)} %copy.31), channel_id=2, replica_groups=mesh['grp'=4,'row'=4,'col'=16] {'row'}, dimensions={2}, use_global_device_ids=true | all-gather | bytes 972800 | tf_op jit(solution)/shard_map/all_gather | solution.py:33
  24.5 80.7 %all-gather.6.cloned.1.call-done = bf16[4,10,64,608]{3,0,1,2:T(4,128)(2,1)} async-done(((bf16[4,10,4,608]{3,0,1,2:T(4,128)(2,1)}), bf16[4,10,64,608]{3,0,1,2:T(4,128)(2,1)}) %all-gather.6.cloned.1.call-update) | async-done | bytes 3112976 | tf_op jit(solution)/shard_map/all_gather | solution.py:36
  105.2 2.5 copy.30
  107.7 5.0 fusion.121
  113.9 66.3 %reduce-scatter.2.cloned.1.call-done = f32[640,640]{1,0:T(8,128)} async-done(((f32[2560,640]{1,0:T(8,128)}), f32[640,640]{1,0:T(8,128)}) %reduce-scatter.2.cloned.1.call-update) | async-done | bytes 1638416 | tf_op jit(solution)/shard_map/reduce_scatter | solution.py:39
  186.4 86.7 %all-gather.8.cloned.1.call-done = f32[16,64,640]{2,0,1:T(8,128)} async-done(((f32[16,4,640]{2,0,1:T(8,128)}), f32[16,64,640]{2,0,1:T(8,128)}) %all-gather.8.cloned.1.call-update) | async-done | bytes 2621456 | tf_op jit(solution)/shard_map/all_gather | solution.py:65
  273.1 2.6 copy.35
  279.1 52.8 %all-gather.10.cloned.1.call-done = f32[1024,1024]{1,0:T(8,128)} async-done(((f32[64,1024]{1,0:T(8,128)}), f32[1024,1024]{1,0:T(8,128)}) %all-gather.10.cloned.1.call-update) | async-done | bytes 4194320 | tf_op jit(solution)/shard_map/all_gather | solution.py:67
  331.9 5.5 copy.37
  337.5 4.4 fusion
  343.8 11.7 %cholesky.223 = f32[128,128]{1,0:T(8,128)S(1)} custom-call(f32[128,128]{1,0:T(8,128)S(1)} %cholesky.580), custom_call_target="Cholesky" | custom-call | tf_op jit(solution)/shard_map/jit(cholesky)/cholesky | solution.py:68
  355.6 9.8 %custom-call.62 = f32[1,128,128]{1,2,0:T(8,128)S(1)} custom-call(f32[1,128,128]{2,1,0:T(8,128)S(1)} %get-tuple-element.103), custom_call_target="InvertDiagBlocksLowerTriangular" | custom-call | tf_op jit(solution)/shard_map/jit(cholesky)/cholesky | solution.py:68
  365.4 2.5 cholesky.255
  371.9 12.1 %cholesky.244 = f32[128,128]{1,0:T(8,128)S(1)} custom-call(f32[128,128]{1,0:T(8,128)S(1)} %cholesky.584), custom_call_target="Cholesky" | custom-call | tf_op jit(solution)/shard_map/jit(cholesky)/cholesky | solution.py:68
  384.6 9.8 %custom-call.63 = f32[1,128,128]{1,2,0:T(8,128)S(1)} custom-call(f32[1,128,128]{2,1,0:T(8,128)S(1)} %get-tuple-element.100), custom_call_target="InvertDiagBlocksLowerTriangular" | custom-call | tf_op jit(solution)/shard_map/jit(cholesky)/cholesky | solution.py:68
  397.8 11.7 %cholesky.468 = f32[128,128]{1,0:T(8,128)S(1)} custom-call(f32[128,128]{1,0:T(8,128)S(1)} %cholesky.589), custom_call_target="Cholesky" | custom-call | tf_op jit(solution)/shard_map/jit(cholesky)/cholesky | solution.py:68
  410.8 9.8 %custom-call.64 = f32[1,128,128]{1,2,0:T(8,128)S(1)} custom-call(f32[1,128,128]{2,1,0:T(8,128)S(1)} %get-tuple-element.97), custom_call_target="InvertDiagBlocksLowerTriangular" | custom-call | tf_op jit(solution)/shard_map/jit(cholesky)/cholesky | solution.py:68
  424.1 11.8 %cholesky.487 = f32[128,128]{1,0:T(8,128)S(1)} custom-call(f32[128,128]{1,0:T(8,128)S(1)} %cholesky.594), custom_call_target="Cholesky" | custom-call | tf_op jit(solution)/shard_map/jit(cholesky)/cholesky | solution.py:68
  437.3 9.8 %custom-call.65 = f32[1,128,128]{1,2,0:T(8,128)S(1)} custom-call(f32[1,128,128]{2,1,0:T(8,128)S(1)} %get-tuple-element.94), custom_call_target="InvertDiagBlocksLowerTriangular" | custom-call | tf_op jit(solution)/shard_map/jit(cholesky)/cholesky | solution.py:68
  450.5 11.7 %cholesky.506 = f32[128,128]{1,0:T(8,128)S(1)} custom-call(f32[128,128]{1,0:T(8,128)S(1)} %cholesky.599), custom_call_target="Cholesky" | custom-call | tf_op jit(solution)/shard_map/jit(cholesky)/cholesky | solution.py:68
  463.6 10.0 %custom-call.66 = f32[1,128,128]{1,2,0:T(8,128)S(1)} custom-call(f32[1,128,128]{2,1,0:T(8,128)S(1)} %get-tuple-element.91), custom_call_target="InvertDiagBlocksLowerTriangular" | custom-call | tf_op jit(solution)/shard_map/jit(cholesky)/cholesky | solution.py:68
  476.9 11.7 %cholesky.526 = f32[128,128]{1,0:T(8,128)S(1)} custom-call(f32[128,128]{1,0:T(8,128)S(1)} %cholesky.604), custom_call_target="Cholesky" | custom-call | tf_op jit(solution)/shard_map/jit(cholesky)/cholesky | solution.py:68
  489.9 9.8 %custom-call.67 = f32[1,128,128]{1,2,0:T(8,128)S(1)} custom-call(f32[1,128,128]{2,1,0:T(8,128)S(1)} %get-tuple-element.88), custom_call_target="InvertDiagBlocksLowerTriangular" | custom-call | tf_op jit(solution)/shard_map/jit(cholesky)/cholesky | solution.py:68
  502.7 12.1 %cholesky.546 = f32[128,128]{1,0:T(8,128)S(1)} custom-call(f32[128,128]{1,0:T(8,128)S(1)} %cholesky.609), custom_call_target="Cholesky" | custom-call | tf_op jit(solution)/shard_map/jit(cholesky)/cholesky | solution.py:68
  516.1 9.8 %custom-call.68 = f32[1,128,128]{1,2,0:T(8,128)S(1)} custom-call(f32[1,128,128]{2,1,0:T(8,128)S(1)} %get-tuple-element.85), custom_call_target="InvertDiagBlocksLowerTriangular" | custom-call | tf_op jit(solution)/shard_map/jit(cholesky)/cholesky | solution.py:68
  528.6 11.7 %cholesky.564 = f32[128,128]{1,0:T(8,128)S(1)} custom-call(f32[128,128]{1,0:T(8,128)S(1)} %convolution_subtract_fusion.18), custom_call_target="Cholesky" | custom-call | tf_op jit(solution)/shard_map/jit(cholesky)/cholesky | solution.py:68
  547.3 4.8 select_select_fusion
  552.1 23.0 %while.4 = (s32[]{:T(128)}, f32[1024,1024]{1,0:T(8,128)}, s32[8,2]{0,1:T(2,128)S(1)}, f32[8,128,128]{2,1,0:T(8,128)S(1)}, s32[]{:T(128)}) while((s32[]{:T(128)}, f32[1024,1024]{1,0:T(8,128)}, s32[8,2]{0,1:T(2,128)S(1)}, f32[8,128,128]{2,1,0:T(8,128)S(1)}, s32[]{:T(128)}) %tuple.84), condition=%wide.while_cond, body=%wide.while_body.sunk | while | flops 2 | bytes 131189 | solution.py:69
  575.1 78.8 %custom-call.70 = f32[8,128,128]{1,2,0:T(8,128)S(1)} custom-call(f32[8,128,128]{2,1,0:T(8,128)S(1)} %get-tuple-element.20), custom_call_target="InvertDiagBlocksLowerTriangular" | custom-call | tf_op jit(solution)/shard_map/jit(_solve_triangular)/triangular_solve | solution.py:69
  674.8 2.7 convolution_subtract_fusion.6
  693.6 2.7 convolution_subtract_fusion.2
  697.9 8.7 %fusion.4 = f32[640,640]{1,0:T(8,128)S(1)} fusion(f32[640,640]{1,0:T(8,128)S(1)} %select_add_fusion, f32[1024,640]{1,0:T(8,128)S(1)} %convolution_dynamic-update-slice_fusion.1, f32[1024,640]{1,0:T(8,128)} %convolution_dynamic-update-slice_fusion.2, pred[640]{0:T(1024)(128)(4,1)S(1)} %broadcast_compare_fusion, pred[640]{0:T(1024)(128)(4,1)S(1)} %broadcast_compare_fusion.1), kind=kOutput, calls=%fused_computation.12 | convolution fusion | flops 5034885120 | bytes 8520960 | tf_op jit(solution)/shard_map/dot_general | solution.py:87
  (153 shorter events, 117.4 us)
Async XLA Ops:
  6.5 1.0 copy-start
  6.5 98.7 %all-gather.6.cloned.1.call-start = ((), (), s32[]{:S(2)}) async-start(), calls=%async_computation.1 | async-start | bytes 3481600 | tf_op jit(solution)/shard_map/all_gather | solution.py:36
  10.8 169.5 %reduce-scatter.2.cloned.1.call-start = ((), (), s32[]{:S(2)}) async-start(), calls=%async_computation.2 | async-start | bytes 8192000 | tf_op jit(solution)/shard_map/reduce_scatter | solution.py:39
  112.7 0.7 copy-start.6
  112.8 160.3 %all-gather.8.cloned.1.call-start = ((), (), s32[]{:S(2)}) async-start(), calls=%async_computation.3 | async-start | bytes 2785280 | tf_op jit(solution)/shard_map/all_gather | solution.py:65
  186.3 145.6 %all-gather.10.cloned.1.call-start = ((), (), s32[]{:S(2)}) async-start(), calls=%async_computation.4 | async-start | bytes 4456448 | tf_op jit(solution)/shard_map/all_gather | solution.py:67
  275.7 1.6 copy-start.2
  278.2 399.3 %all-gather.12.cloned.1.call-start = ((), (), s32[]{:S(2)}) async-start(), calls=%async_computation.5 | async-start | bytes 2785280 | tf_op jit(solution)/shard_map/all_gather | solution.py:72
  341.9 1.9 copy-start.4
  653.9 5.1 copy-start.3
  677.5 3.6 copy-start.5
  710.0 3.3 copy-start.1
Sparse Core Ops, SparseCore 0:
  10.9 94.2 all-gather.5
  112.9 67.3 reduce-scatter.1
  186.4 86.6 all-gather.7
  278.3 53.5 all-gather.9
  333.6 51.7 all-gather.11
where the time goes:
time: 727 us; the launch traced here: 720 us
  waiting for transfers between devices  287 us (39%)
  other arithmetic  266 us (37%)
  matrix products  82.7 us (11%)
  local copies, waits for them, and re-layouts  51.7 us (7%)
  between operations  19.2 us (3%)
  blocking collectives  13.4 us (2%)
    another operation x30, other arithmetic, local(): cholesky_factor = jnp.linalg.cholesky(diagonal_block)  173 us
    all_gather x1, waiting for transfers between devices, local(): lax.all_gather(own_panel, 'col', axis=1, tiled=True).reshape(PW, local_rows)  86.7 us
    another operation x4, other arithmetic, local(): jax.scipy.linalg.solve_triangular(cholesky_factor, panel_cols_t, lower=True)  83.6 us
    all_gather x1, waiting for transfers between devices, local(): lax.all_gather(whitened, 'col', axis=2, tiled=True)  80.7 us
    reduce_scatter x1, waiting for transfers between devices, local(): lax.psum_scatter(lax.dot_general(row_side, col_side, (((1,), (1,)), ((),...  66.3 us
    all_gather x1, waiting for transfers between devices, local(): lax.all_gather(own_piece, ('grp', 'row'), axis=0, tiled=True)  52.8 us
    another operation x15, matrix products, local(): jax.scipy.linalg.solve_triangular(cholesky_factor, panel_cols_t, lower=True)  24.7 us
    another operation x14, matrix products, local(): cholesky_factor = jnp.linalg.cholesky(diagonal_block)  23.1 us
  transfers between devices with their start and end apart: 5, of which 4 were waited for; matrix products, arithmetic and copies ran while one was open for 47% of the time, Pallas kernels for 0%

commit v1 on v0

v1 whole, which is shorter than its diff:
```python
import jax
import jax.numpy as jnp
from jax import lax
from jax.sharding import PartitionSpec as P

PW = 1024
PANELS = 1
NPAN = 10


def local(block_rows, inverse_factor, live_rows, shift):
    highest = lax.Precision.HIGHEST
    groups = lax.axis_size("grp")
    rowcount = lax.axis_size("row")
    colcount = lax.axis_size("col")
    owners = groups * rowcount
    slab = PW // owners
    window = slab // colcount
    group_index = lax.axis_index("grp")
    row_index = lax.axis_index("row")
    col_index = lax.axis_index("col")
    blocks, padded, local_cols = block_rows.shape
    stacked = blocks * padded
    total = stacked * groups
    n_all = NPAN * owners * slab

    ordinal = jnp.arange(padded, dtype=jnp.int32)
    live_mask = (ordinal[None, :] < live_rows[:, None]).astype(jnp.float32)
    masked_factor = inverse_factor * live_mask[:, :, None] * live_mask[:, None, :]
    whitened = jnp.einsum(
        "bij,bjm->mbi", masked_factor, block_rows.astype(jnp.float32), precision=highest
    )
    whitened = whitened.astype(jnp.bfloat16).reshape(local_cols, stacked)

    every = lax.all_gather(whitened, "grp", axis=0, tiled=False)
    every = jnp.transpose(every, (1, 0, 2)).reshape(groups, NPAN, window, total)

    panel_w = every[:, 0]
    panel_w = lax.all_gather(panel_w, "col", axis=0, tiled=False)
    panel_w = lax.all_gather(panel_w, "row", axis=0, tiled=False)
    every, panel_w = lax.optimization_barrier((every, panel_w))
    panel_w = jnp.transpose(panel_w, (2, 0, 1, 3, 4)).reshape(PW, total)

    row_w = lax.dynamic_index_in_dim(every, group_index, 0, keepdims=False)
    row_w = lax.all_gather(row_w, "col", axis=0, tiled=False)
    row_w = jnp.transpose(row_w, (1, 0, 2, 3)).reshape(NPAN * colcount * window, total)

    col_w = lax.all_gather(every, "row", axis=0, tiled=False)
    col_w = jnp.transpose(col_w, (2, 1, 0, 3, 4)).reshape(NPAN * owners * window, total)

    shift_all = lax.all_gather(shift, ("grp", "row", "col"), axis=0, tiled=True)
    shift_nat = jnp.transpose(
        shift_all.reshape(groups, rowcount, colcount, NPAN, window), (3, 0, 1, 2, 4)
    ).reshape(n_all)

    panel_ids = jnp.arange(NPAN, dtype=jnp.int32)
    slab_ids = jnp.arange(slab, dtype=jnp.int32)
    owner_ids = jnp.arange(owners, dtype=jnp.int32)
    window_ids = jnp.arange(window, dtype=jnp.int32)
    own_owner = group_index * rowcount + row_index
    row_global = ((panel_ids[:, None] * owners + own_owner) * slab + slab_ids[None, :]).reshape(-1)
    col_global = (
        (panel_ids[:, None, None] * owners + owner_ids[None, :, None]) * slab
        + col_index * window
        + window_ids[None, None, :]
    ).reshape(-1)
    panel_ids_all = jnp.arange(PW, dtype=jnp.int32)
    shift_panel = shift_nat[:PW]

    dims = (((1,), (1,)), ((), ()))
    f32 = jnp.float32
    diag_block = lax.dot_general(panel_w, panel_w, dims, preferred_element_type=f32)
    diag_block = diag_block + jnp.where(
        panel_ids_all[:, None] == panel_ids_all[None, :], shift_panel[None, :], 0.0
    )
    both_w = jnp.concatenate([row_w, col_w], axis=0)
    both_global = jnp.concatenate([row_global, col_global], axis=0)
    both_panel = lax.dot_general(both_w, panel_w, dims, preferred_element_type=f32)
    both_panel = both_panel + jnp.where(
        both_global[:, None] == panel_ids_all[None, :], shift_panel[None, :], 0.0
    )
    schur_tile = lax.dot_general(row_w, col_w, dims, preferred_element_type=f32)
    schur_tile = schur_tile + jnp.where(
        row_global[:, None] == col_global[None, :], shift_nat[col_global][None, :], 0.0
    )

    cholesky_factor = jnp.linalg.cholesky(diag_block)
    solved = lax.linalg.triangular_solve(
        cholesky_factor, both_panel, left_side=False, lower=True, transpose_a=True
    )
    local_rows = row_global.shape[0]
    row_factor = solved[:local_rows]
    col_factor = solved[local_rows:]

    panel_piece = lax.dynamic_slice_in_dim(
        row_factor.reshape(local_rows, owners, slab), col_index * window, window, 2
    ).reshape(local_rows, owners * window)
    panel_cols_global = col_global.reshape(NPAN, -1)[0]
    finished = jnp.where(row_global[:, None] >= panel_cols_global[None, :], panel_piece, 0.0)

    boundary = PANELS * PW
    first_trailing = owners * window
    update = jnp.dot(
        row_factor, col_factor[first_trailing:].T, precision=highest, preferred_element_type=f32
    )
    trailing = schur_tile[:, first_trailing:] - update
    trailing = jnp.where(row_global[:, None] >= boundary, trailing, 0.0)
    return jnp.concatenate([finished, trailing], axis=1)


def solution(mesh):
    in_specs = (
        P("grp", None, ("row", "col")),
        P("grp", None, None),
        P("grp"),
        P(("grp", "row", "col")),
    )
    out_specs = P(("grp", "row"), "col")
    return jax.shard_map(local, mesh=mesh, in_specs=in_specs, out_specs=out_specs, check_vma=False)
```

time: 727 us -> 648 us (0.89)
  waiting for transfers between devices: 287 us -> 79 us
  blocking collectives: 13.4 us -> 88.7 us
  local copies, waits for them, and re-layouts: 51.7 us -> 83.2 us
  matrix products: 82.7 us -> 105 us
    all_gather x4, waiting for transfers between devices: 220 us -> 78.9 us  [the longest x1 78.9 us: local(): panel_w = lax.all_gather(panel_w, 'col', axis=0, tiled=False)]
    unnamed x0 -> x1, blocking collectives: none -> 78.3 us
    reduce_scatter x1 -> x0, waiting for transfers between devices: 66.3 us -> none  [local(): lax.psum_scatter(lax.dot_general(row_side, col_side, (((1,), (1,)), ((),...]
    dot_general x2 -> x4, matrix products: 13.7 us -> 35.7 us  [the longest x1 10.9 us: local(): lax.dot_general(panel_w, panel_w, dims, preferred_element_type=f32)]
    reshape x5 -> x7, local copies, waits for them, and re-layouts: 4.4 us -> 18.2 us  [the longest x1 8.71 us: local(): panel_w = jnp.transpose(panel_w, (2, 0, 1, 3, 4)).reshape(PW, total)]
    all_gather x4 -> x1, local copies, waits for them, and re-layouts: 10.7 us -> 3.13 us  [local(): col_w = lax.all_gather(every, 'row', axis=0, tiled=False)]
    another operation x33 -> x34, local copies, waits for them, and re-layouts: 25.4 us -> 30.2 us  [the longest x25 22.8 us: local(): jax.scipy.linalg.solve_triangular(cholesky_factor, panel_cols_t, lower=True)]
    another operation x34 -> x33, other arithmetic: 256 us -> 257 us  [the longest x30 172 us: local(): cholesky_factor = jnp.linalg.cholesky(diag_block)]
  transfers between devices with their start and end apart: 5 -> 4, of which waited for: 4 -> 1; matrix products, arithmetic and copies ran while one was open for 47% -> 55% of each run, Pallas kernels for 0% -> 0%
where the time goes in v1:
time: 648 us; the launch traced here: 639 us
  other arithmetic  263 us (41%)
  matrix products  105 us (16%)
  blocking collectives  88.7 us (14%)
  local copies, waits for them, and re-layouts  83.2 us (13%)
  waiting for transfers between devices  79 us (12%)
  between operations  19.1 us (3%)
    another operation x30, other arithmetic, local(): cholesky_factor = jnp.linalg.cholesky(diag_block)  172 us
    another operation x3, other arithmetic, local(): lax.linalg.triangular_solve(cholesky_factor, both_panel, left_side=False,...  85 us
    all_gather x1, waiting for transfers between devices, local(): panel_w = lax.all_gather(panel_w, 'col', axis=0, tiled=False)  78.9 us
    unnamed x1, blocking collectives  78.3 us
    another operation x15, matrix products, local(): lax.linalg.triangular_solve(cholesky_factor, both_panel, left_side=False,...  44.5 us
    another operation x24, local copies, waits for them, and re-layouts  27.4 us
    another operation x14, matrix products, local(): cholesky_factor = jnp.linalg.cholesky(diag_block)  23.1 us
  transfers between devices with their start and end apart: 4, of which 1 were waited for; matrix products, arithmetic and copies ran while one was open for 55% of the time, Pallas kernels for 0%

profile of v1, /device:TPU:1, one launch (start us, length us, event | category | flops | bytes accessed | tf_op | source)
XLA Modules:
  0.0 638.7 jit_solution(12855038742688722585)
XLA Ops:
  10.0 10.4 %all_gather.25 = bf16[4,160,608]{2,1,0:T(8,128)(2,1)S(1)} all-gather(bf16[1,160,608]{2,1,0:T(8,128)(2,1)S(1)} %all_gather_reshape.3), channel_id=1, replica_groups=mesh['grp'=4,'row'=4,'col'=16] {'grp'}, dimensions={0}, use_global_device_ids=true | all-gather | bytes 972800 | tf_op jit(solution)/shard_map/all_gather | solution.py:35
  22.5 78.9 %all-gather.10.cloned.1.call-done = bf16[64,1,4,2432]{3,2,1,0:T(4,128)(2,1)} async-done(((bf16[4,1,4,2432]{3,2,1,0:T(4,128)(2,1)}), bf16[64,1,4,2432]{3,2,1,0:T(4,128)(2,1)}) %all-gather.10.cloned.1.call-update) | async-done | bytes 1245200 | tf_op jit(solution)/shard_map/all_gather | solution.py:39
  102.4 78.3 %all-reduce.1 = f32[10240]{0:T(1024)S(1)} all-reduce(f32[10240]{0:T(1024)S(1)} %dynamic-update-slice.47), channel_id=1, replica_groups=mesh['grp'=4,'row'=4,'col'=16] {'grp','row','col'}, use_global_device_ids=true, to_apply=%add.1 | all-reduce | flops 10240 | bytes 81920
  189.3 7.0 %copy.25 = bf16[4,16,4,4,2432]{4,3,1,0,2:T(4,128)(2,1)} copy(bf16[4,16,4,4,2432]{4,3,2,1,0:T(4,128)(2,1)} %bitcast.134) | data formatting | bytes 9961472 | tf_op jit(solution)/shard_map/optimization_barrier | solution.py:41
  196.3 8.7 %reshape.253 = bf16[1024,2432]{1,0:T(8,128)(2,1)} reshape(bf16[4,4,16,4,2432]{4,3,2,1,0:T(4,128)(2,1)} %bitcast.130) | data formatting | bytes 9961472 | tf_op jit(solution)/shard_map/reshape | solution.py:42
  205.1 10.9 %fusion.87 = f32[1024,1024]{1,0:T(8,128)} fusion(bf16[1024,2432]{1,0:T(8,128)(2,1)} %reshape.253), kind=kOutput, calls=%fused_computation.197 | convolution fusion | flops 5100273664 | bytes 9175040 | tf_op jit(solution)/shard_map/dot_general | solution.py:72
  216.0 5.5 copy.20
  228.2 11.7 %cholesky.222 = f32[128,128]{1,0:T(8,128)S(1)} custom-call(f32[128,128]{1,0:T(8,128)S(1)} %cholesky.577), custom_call_target="Cholesky" | custom-call | tf_op jit(solution)/shard_map/jit(cholesky)/cholesky | solution.py:87
  242.5 9.8 %custom-call.62 = f32[1,128,128]{1,2,0:T(8,128)S(1)} custom-call(f32[1,128,128]{2,1,0:T(8,128)S(1)} %get-tuple-element.73), custom_call_target="InvertDiagBlocksLowerTriangular" | custom-call | tf_op jit(solution)/shard_map/jit(cholesky)/cholesky | solution.py:87
  256.2 11.9 %cholesky.243 = f32[128,128]{1,0:T(8,128)S(1)} custom-call(f32[128,128]{1,0:T(8,128)S(1)} %cholesky.581), custom_call_target="Cholesky" | custom-call | tf_op jit(solution)/shard_map/jit(cholesky)/cholesky | solution.py:87
  268.8 9.8 %custom-call.63 = f32[1,128,128]{1,2,0:T(8,128)S(1)} custom-call(f32[1,128,128]{2,1,0:T(8,128)S(1)} %get-tuple-element.70), custom_call_target="InvertDiagBlocksLowerTriangular" | custom-call | tf_op jit(solution)/shard_map/jit(cholesky)/cholesky | solution.py:87
  282.0 11.7 %cholesky.466 = f32[128,128]{1,0:T(8,128)S(1)} custom-call(f32[128,128]{1,0:T(8,128)S(1)} %cholesky.586), custom_call_target="Cholesky" | custom-call | tf_op jit(solution)/shard_map/jit(cholesky)/cholesky | solution.py:87
  294.3 9.8 %custom-call.64 = f32[1,128,128]{1,2,0:T(8,128)S(1)} custom-call(f32[1,128,128]{2,1,0:T(8,128)S(1)} %get-tuple-element.67), custom_call_target="InvertDiagBlocksLowerTriangular" | custom-call | tf_op jit(solution)/shard_map/jit(cholesky)/cholesky | solution.py:87
  307.7 12.1 %cholesky.485 = f32[128,128]{1,0:T(8,128)S(1)} custom-call(f32[128,128]{1,0:T(8,128)S(1)} %cholesky.591), custom_call_target="Cholesky" | custom-call | tf_op jit(solution)/shard_map/jit(cholesky)/cholesky | solution.py:87
  320.4 9.8 %custom-call.65 = f32[1,128,128]{1,2,0:T(8,128)S(1)} custom-call(f32[1,128,128]{2,1,0:T(8,128)S(1)} %get-tuple-element.64), custom_call_target="InvertDiagBlocksLowerTriangular" | custom-call | tf_op jit(solution)/shard_map/jit(cholesky)/cholesky | solution.py:87
  333.7 11.7 %cholesky.504 = f32[128,128]{1,0:T(8,128)S(1)} custom-call(f32[128,128]{1,0:T(8,128)S(1)} %cholesky.596), custom_call_target="Cholesky" | custom-call | tf_op jit(solution)/shard_map/jit(cholesky)/cholesky | solution.py:87
  346.0 10.0 %custom-call.66 = f32[1,128,128]{1,2,0:T(8,128)S(1)} custom-call(f32[1,128,128]{2,1,0:T(8,128)S(1)} %get-tuple-element.61), custom_call_target="InvertDiagBlocksLowerTriangular" | custom-call | tf_op jit(solution)/shard_map/jit(cholesky)/cholesky | solution.py:87
  361.0 11.7 %cholesky.524 = f32[128,128]{1,0:T(8,128)S(1)} custom-call(f32[128,128]{1,0:T(8,128)S(1)} %cholesky.601), custom_call_target="Cholesky" | custom-call | tf_op jit(solution)/shard_map/jit(cholesky)/cholesky | solution.py:87
  373.3 9.8 %custom-call.67 = f32[1,128,128]{1,2,0:T(8,128)S(1)} custom-call(f32[1,128,128]{2,1,0:T(8,128)S(1)} %get-tuple-element.58), custom_call_target="InvertDiagBlocksLowerTriangular" | custom-call | tf_op jit(solution)/shard_map/jit(cholesky)/cholesky | solution.py:87
  386.2 12.1 %cholesky.544 = f32[128,128]{1,0:T(8,128)S(1)} custom-call(f32[128,128]{1,0:T(8,128)S(1)} %cholesky.606), custom_call_target="Cholesky" | custom-call | tf_op jit(solution)/shard_map/jit(cholesky)/cholesky | solution.py:87
  398.9 9.8 %custom-call.68 = f32[1,128,128]{1,2,0:T(8,128)S(1)} custom-call(f32[1,128,128]{2,1,0:T(8,128)S(1)} %get-tuple-element.55), custom_call_target="InvertDiagBlocksLowerTriangular" | custom-call | tf_op jit(solution)/shard_map/jit(cholesky)/cholesky | solution.py:87
  411.3 11.7 %cholesky.562 = f32[128,128]{1,0:T(8,128)S(1)} custom-call(f32[128,128]{1,0:T(8,128)S(1)} %convolution_subtract_fusion.12), custom_call_target="Cholesky" | custom-call | tf_op jit(solution)/shard_map/jit(cholesky)/cholesky | solution.py:87
  433.3 4.9 select_select_fusion
  438.3 27.4 %while.1 = (s32[]{:T(128)}, f32[1024,1024]{1,0:T(8,128)}, s32[8,2]{0,1:T(2,128)S(1)}, f32[8,128,128]{2,1,0:T(8,128)}, s32[]{:T(128)}) while((s32[]{:T(128)}, f32[1024,1024]{1,0:T(8,128)}, s32[8,2]{0,1:T(2,128)S(1)}, f32[8,128,128]{2,1,0:T(8,128)}, s32[]{:T(128)}) %tuple.59), condition=%wide.while_cond, body=%wide.while_body.sunk | while | flops 2 | bytes 132205 | solution.py:88
  465.7 80.0 %custom-call.69 = f32[8,128,128]{1,2,0:T(8,128)} custom-call(f32[8,128,128]{2,1,0:T(8,128)} %get-tuple-element.16), custom_call_target="InvertDiagBlocksLowerTriangular" | custom-call | tf_op jit(solution)/shard_map/triangular_solve | solution.py:88
  558.1 5.7 fusion.88
  563.8 9.7 %select_add_fusion = f32[1280,1024]{1,0:T(8,128)S(1)} fusion(bf16[1024,2432]{1,0:T(8,128)(2,1)} %reshape.253, bf16[640,2432]{1,0:T(8,128)(2,1)S(1)} %copy-done.5, bf16[640,2432]{1,0:T(8,128)(2,1)S(1)} %copy-done.6, f32[1024]{0:T(1024)S(1)} %broadcast_in_dim.75, s32[1280]{0:T(1024)S(1)} %pad_add_fusion), kind=kOutput, calls=%fused_computation.7 | convolution fusion | flops 6391726080 | bytes 16458752 | tf_op jit(solution)/shard_map/dot_general | solution.py:78
  586.5 5.3 fusion.18
  592.6 7.0 %convolution_subtract_fusion = f32[1280,128]{1,0:T(8,128)S(1)} fusion(f32[1280,640]{0,1:T(8,128)S(1)} %get-tuple-element.35, f32[1280,1024]{1,0:T(8,128)S(1)} %select_add_fusion, f32[1024,1024]{1,0:T(8,128)} %get-tuple-element.130), kind=kOutput, calls=%fused_computation.29 | convolution fusion | flops 1258455040 | bytes 4915200 | tf_op jit(solution)/shard_map/triangular_solve | solution.py:88
  600.4 7.5 %convolution_subtract_fusion.1 = f32[1280,128]{1,0:T(8,128)S(1)} fusion(f32[1280,768]{0,1:T(8,128)S(1)} %get-tuple-element.31, f32[1280,1024]{1,0:T(8,128)S(1)} %select_add_fusion, f32[1024,1024]{1,0:T(8,128)} %get-tuple-element.130), kind=kOutput, calls=%fused_computation.31 | convolution fusion | flops 1510113280 | bytes 5636096 | tf_op jit(solution)/shard_map/triangular_solve | solution.py:88
  608.5 8.8 %convolution_subtract_fusion.5 = f32[1280,128]{1,0:T(8,128)S(1)} fusion(f32[1280,896]{0,1:T(8,128)S(1)} %get-tuple-element.27, f32[1280,1024]{1,0:T(8,128)S(1)} %select_add_fusion, f32[1024,1024]{1,0:T(8,128)} %get-tuple-element.130), kind=kOutput, calls=%fused_computation.35 | convolution fusion | flops 1761771520 | bytes 6356992 | tf_op jit(solution)/shard_map/triangular_solve | solution.py:88
  620.7 9.4 %fusion.27 = f32[640,576]{0,1:T(8,128)S(1)} fusion(f32[640,640]{0,1:T(8,128)S(1)} %fusion.88, f32[1280,1024]{0,1:T(8,128)} %copy-done.2, f32[576]{0:T(1024)S(1)} %slice.269, s32[640]{0:T(1024)S(1)} %add.213, s32[576]{0:T(1024)S(1)} %slice.268, pred[640]{0:T(1024)(128)(4,1)S(1)} %broadcast_compare_fusion), kind=kOutput, calls=%fused_computation.44 | convolution fusion | flops 4531691520 | bytes 8199808 | tf_op jit(solution)/shard_map/dot_general | solution.py:103
  (147 shorter events, 118.2 us)
Async XLA Ops:
  6.5 1.0 copy-start
  6.5 94.8 %all-gather.10.cloned.1.call-start = ((), (), s32[]{:S(2)}) async-start(), calls=%async_computation.1 | async-start | bytes 1323008 | tf_op jit(solution)/shard_map/all_gather | solution.py:39
  7.5 94.7 %copy-start.8 = (f32[40]{0:T(128)S(1)}, f32[40]{0:T(128)}, u32[]{:S(2)}) copy-start(f32[40]{0:T(128)} %param.7) | copy-start | bytes 484
  21.6 163.2 %copy-start.4 = (bf16[4,10,4,2432]{3,2,1,0:T(4,128)(2,1)}, bf16[4,10,4,2432]{3,2,1,0:T(4,128)(2,1)S(1)}, u32[]{:S(2)}) copy-start(bf16[4,10,4,2432]{3,2,1,0:T(4,128)(2,1)S(1)} %reshape.250) | copy-start | bytes 2334724
  22.4 166.9 %all-gather.12.cloned.1.call-start = ((), (), s32[]{:S(2)}) async-start(), calls=%async_computation.2 | async-start | bytes 6225920 | tf_op jit(solution)/shard_map/all_gather | solution.py:40
  101.4 444.3 %all-gather.14.cloned.1.call-start = ((), (), s32[]{:S(2)}) async-start(), calls=%async_computation.3 | async-start | bytes 3891200 | tf_op jit(solution)/shard_map/all_gather | solution.py:48
  205.0 346.8 %all-gather.8.cloned.1.call-start = ((), (), s32[]{:S(2)}) async-start(), calls=%async_computation | async-start | bytes 3307520 | tf_op jit(solution)/shard_map/all_gather | solution.py:45
  226.2 2.0 copy-start.3
  558.1 5.7 copy-start.5
  558.1 5.7 copy-start.6
  563.8 9.7 %copy-start.7 = (f32[8,128,128]{1,2,0:T(8,128)S(1)}, f32[8,128,128]{1,2,0:T(8,128)}, u32[]{:S(2)}) copy-start(f32[8,128,128]{1,2,0:T(8,128)} %custom-call.69) | copy-start | bytes 1572868
  618.1 2.3 copy-start.2
  620.7 11.3 %copy-start.1 = (bf16[2,304,160]{1,2,0:T(8,128)(2,1)S(1)}, bf16[2,304,160]{1,2,0:T(8,128)(2,1)}, u32[]{:S(2)}) copy-start(bf16[2,304,160]{1,2,0:T(8,128)(2,1)} %param.4) | copy-start | bytes 583684
Sparse Core Ops, SparseCore 0:
  22.5 78.7 all-gather.9
  103.2 57.9 all-gather.11
  205.1 37.4 all-gather.13
  357.8 85.3 all-gather.7

commit v2 on v1

--- a/solution.py
+++ b/solution.py
@@ -6,6 +6,19 @@
 PW = 1024
 PANELS = 1
 NPAN = 10
+
+
+def split3(x):
+    hi = lax.reduce_precision(x, exponent_bits=8, mantissa_bits=7)
+    rest = x - hi
+    mid = lax.reduce_precision(rest, exponent_bits=8, mantissa_bits=7)
+    lo = rest - mid
+    return jnp.concatenate([hi, mid, lo]).astype(jnp.bfloat16)
+
+
+def join3(parts):
+    parts = parts.astype(jnp.float32).reshape(parts.shape[:-1] + (3, -1))
+    return (parts[..., 0, :] + parts[..., 1, :]) + parts[..., 2, :]
 
 
 def local(block_rows, inverse_factor, live_rows, shift):
@@ -22,7 +35,6 @@
     blocks, padded, local_cols = block_rows.shape
     stacked = blocks * padded
     total = stacked * groups
-    n_all = NPAN * owners * slab
 
     ordinal = jnp.arange(padded, dtype=jnp.int32)
     live_mask = (ordinal[None, :] < live_rows[:, None]).astype(jnp.float32)
@@ -32,13 +44,27 @@
     )
     whitened = whitened.astype(jnp.bfloat16).reshape(local_cols, stacked)
 
-    every = lax.all_gather(whitened, "grp", axis=0, tiled=False)
-    every = jnp.transpose(every, (1, 0, 2)).reshape(groups, NPAN, window, total)
+    shift_row = jnp.zeros((1, stacked), jnp.bfloat16).at[0, : 3 * shift.shape[0]].set(
+        split3(shift)
+    )
+    every = lax.all_gather(
+        jnp.concatenate([whitened, shift_row], axis=0), "grp", axis=0, tiled=False
+    )
+    shift_grp = join3(every[:, local_cols, : 3 * shift.shape[0]]).reshape(groups, NPAN, window)
+    every = jnp.transpose(every[:, :local_cols], (1, 0, 2)).reshape(groups, NPAN, window, total)
 
-    panel_w = every[:, 0]
+    panel_shift_row = jnp.zeros((1, total), jnp.bfloat16).at[0, : 3 * groups * window].set(
+        split3(shift_grp[:, 0].reshape(-1))
+    )
+    panel_w = jnp.concatenate([every[:, 0].reshape(groups * window, total), panel_shift_row], 0)
     panel_w = lax.all_gather(panel_w, "col", axis=0, tiled=False)
     panel_w = lax.all_gather(panel_w, "row", axis=0, tiled=False)
     every, panel_w = lax.optimization_barrier((every, panel_w))
+    shift_panel = join3(panel_w[:, :, groups * window, : 3 * groups * window])
+    shift_panel = jnp.transpose(
+        shift_panel.reshape(rowcount, colcount, groups, window), (2, 0, 1, 3)
+    ).reshape(PW)
+    panel_w = panel_w[:, :, : groups * window].reshape(rowcount, colcount, groups, window, total)
     panel_w = jnp.transpose(panel_w, (2, 0, 1, 3, 4)).reshape(PW, total)
 
     row_w = lax.dynamic_index_in_dim(every, group_index, 0, keepdims=False)
@@ -47,11 +73,6 @@
 
     col_w = lax.all_gather(every, "row", axis=0, tiled=False)
     col_w = jnp.transpose(col_w, (2, 1, 0, 3, 4)).reshape(NPAN * owners * window, total)
-
-    shift_all = lax.all_gather(shift, ("grp", "row", "col"), axis=0, tiled=True)
-    shift_nat = jnp.transpose(
-        shift_all.reshape(groups, rowcount, colcount, NPAN, window), (3, 0, 1, 2, 4)
-    ).reshape(n_all)
 
     panel_ids = jnp.arange(NPAN, dtype=jnp.int32)
     slab_ids = jnp.arange(slab, dtype=jnp.int32)
@@ -65,7 +86,9 @@
         + window_ids[None, None, :]
     ).reshape(-1)
     panel_ids_all = jnp.arange(PW, dtype=jnp.int32)
-    shift_panel = shift_nat[:PW]
+    shift_col = jnp.broadcast_to(
+        shift.reshape(NPAN, 1, window), (NPAN, owners, window)
+    ).reshape(-1)
 
     dims = (((1,), (1,)), ((), ()))
     f32 = jnp.float32
@@ -81,7 +104,7 @@
     )
     schur_tile = lax.dot_general(row_w, col_w, dims, preferred_element_type=f32)
     schur_tile = schur_tile + jnp.where(
-        row_global[:, None] == col_global[None, :], shift_nat[col_global][None, :], 0.0
+        row_global[:, None] == col_global[None, :], shift_col[None, :], 0.0
     )
 
     cholesky_factor = jnp.linalg.cholesky(diag_block)

time: 648 us -> 633 us (0.977)
  blocking collectives: 88.7 us -> 10.5 us
  waiting for transfers between devices: 79 us -> 142 us
    unnamed x1 -> x0, blocking collectives: 78.3 us -> none
    all_gather x1, waiting for transfers between devices: 0.02 us -> 59.4 us  [local(): panel_w = lax.all_gather(panel_w, 'row', axis=0, tiled=False)]
    optimization_barrier x1 -> x0, local copies, waits for them, and re-layouts: 6.96 us -> none  [local(): every, panel_w = lax.optimization_barrier((every, panel_w))]
    another operation x25 -> x26, local copies, waits for them, and re-layouts: 27.6 us -> 22.4 us
    another operation x30 -> x31, other arithmetic: 172 us -> 173 us  [local(): cholesky_factor = jnp.linalg.cholesky(diag_block)]
  transfers between devices with their start and end apart: 4 -> 4, of which waited for: 1 -> 2; matrix products, arithmetic and copies ran while one was open for 55% -> 57% of each run, Pallas kernels for 0% -> 0%
where the time goes in v2:
time: 633 us; the launch traced here: 624 us
  other arithmetic  267 us (42%)
  waiting for transfers between devices  142 us (22%)
  matrix products  105 us (17%)
  local copies, waits for them, and re-layouts  78.8 us (12%)
  between operations  19.1 us (3%)
  blocking collectives  10.5 us (2%)
    another operation x31, other arithmetic, local(): cholesky_factor = jnp.linalg.cholesky(diag_block)  173 us
    another operation x3, other arithmetic, local(): lax.linalg.triangular_solve(cholesky_factor, both_panel, left_side=False,...  84.1 us
    all_gather x1, waiting for transfers between devices, local(): panel_w = lax.all_gather(panel_w, 'col', axis=0, tiled=False)  82.6 us
    all_gather x1, waiting for transfers between devices, local(): panel_w = lax.all_gather(panel_w, 'row', axis=0, tiled=False)  59.4 us
    another operation x15, matrix products, local(): lax.linalg.triangular_solve(cholesky_factor, both_panel, left_side=False,...  44.5 us
    another operation x14, matrix products, local(): cholesky_factor = jnp.linalg.cholesky(diag_block)  23.2 us
    another operation x24, local copies, waits for them, and re-layouts  22.3 us
  transfers between devices with their start and end apart: 4, of which 2 were waited for; matrix products, arithmetic and copies ran while one was open for 57% of the time, Pallas kernels for 0%

profile of v2, /device:TPU:1, one launch (start us, length us, event | category | flops | bytes accessed | tf_op | source)
XLA Modules:
  0.0 623.6 jit_solution(9894235277035679239)
XLA Ops:
  11.9 10.5 %all-gather.4 = bf16[4,161,608]{2,1,0:T(8,128)(2,1)S(1)} all-gather(bf16[1,161,608]{2,1,0:T(8,128)(2,1)S(1)} %fusion.61), channel_id=2, replica_groups=mesh['grp'=4,'row'=4,'col'=16] {'grp'}, dimensions={0}, use_global_device_ids=true | all-gather | bytes 978880 | tf_op jit(solution)/shard_map/all_gather | solution.py:50
  25.6 82.6 %all-gather.17.cloned.1.call-done = bf16[16,17,2432]{2,1,0:T(8,128)(2,1)} async-done(((bf16[1,17,2432]{2,1,0:T(8,128)(2,1)}), bf16[16,17,2432]{2,1,0:T(8,128)(2,1)}) %all-gather.17.cloned.1.call-update) | async-done | bytes 1323024 | tf_op jit(solution)/shard_map/all_gather | solution.py:60
  112.0 59.4 %all-gather.13.cloned.1.call-done = bf16[64,17,2432]{2,0,1:T(8,128)(2,1)} async-done(((bf16[16,17,2432]{2,0,1:T(8,128)(2,1)}), bf16[64,17,2432]{2,0,1:T(8,128)(2,1)}) %all-gather.13.cloned.1.call-update) | async-done | bytes 5292048 | tf_op jit(solution)/shard_map/all_gather | solution.py:61
  172.2 5.0 slice.314
  177.2 8.6 %copy.29 = bf16[4,16,4,4,2432]{4,3,1,0,2:T(4,128)(2,1)} copy(bf16[4,16,4,4,2432]{4,1,0,3,2:T(8,128)(2,1)} %bitcast.151) | data formatting | bytes 9961472 | tf_op jit(solution)/shard_map/reshape | solution.py:67
  185.8 8.8 %reshape.368 = bf16[1024,2432]{1,0:T(8,128)(2,1)} reshape(bf16[4,4,16,4,2432]{4,3,2,1,0:T(4,128)(2,1)} %bitcast.152) | data formatting | bytes 9961472 | tf_op jit(solution)/shard_map/reshape | solution.py:68
  195.2 10.9 %fusion.102 = f32[1024,1024]{1,0:T(8,128)} fusion(bf16[1024,2432]{1,0:T(8,128)(2,1)} %reshape.368), kind=kOutput, calls=%fused_computation.230 | convolution fusion | flops 5100273664 | bytes 9175040 | tf_op jit(solution)/shard_map/dot_general | solution.py:95
  206.1 5.6 copy.25
  218.2 11.7 %cholesky.222 = f32[128,128]{1,0:T(8,128)S(1)} custom-call(f32[128,128]{1,0:T(8,128)S(1)} %cholesky.577), custom_call_target="Cholesky" | custom-call | tf_op jit(solution)/shard_map/jit(cholesky)/cholesky | solution.py:110
  229.9 9.8 %custom-call.62 = f32[1,128,128]{1,2,0:T(8,128)S(1)} custom-call(f32[1,128,128]{2,1,0:T(8,128)S(1)} %get-tuple-element.97), custom_call_target="InvertDiagBlocksLowerTriangular" | custom-call | tf_op jit(solution)/shard_map/jit(cholesky)/cholesky | solution.py:110
  246.2 11.9 %cholesky.243 = f32[128,128]{1,0:T(8,128)S(1)} custom-call(f32[128,128]{1,0:T(8,128)S(1)} %cholesky.581), custom_call_target="Cholesky" | custom-call | tf_op jit(solution)/shard_map/jit(cholesky)/cholesky | solution.py:110
  258.7 9.8 %custom-call.63 = f32[1,128,128]{1,2,0:T(8,128)S(1)} custom-call(f32[1,128,128]{2,1,0:T(8,128)S(1)} %get-tuple-element.94), custom_call_target="InvertDiagBlocksLowerTriangular" | custom-call | tf_op jit(solution)/shard_map/jit(cholesky)/cholesky | solution.py:110
  271.9 11.7 %cholesky.466 = f32[128,128]{1,0:T(8,128)S(1)} custom-call(f32[128,128]{1,0:T(8,128)S(1)} %cholesky.586), custom_call_target="Cholesky" | custom-call | tf_op jit(solution)/shard_map/jit(cholesky)/cholesky | solution.py:110
  284.3 9.8 %custom-call.64 = f32[1,128,128]{1,2,0:T(8,128)S(1)} custom-call(f32[1,128,128]{2,1,0:T(8,128)S(1)} %get-tuple-element.91), custom_call_target="InvertDiagBlocksLowerTriangular" | custom-call | tf_op jit(solution)/shard_map/jit(cholesky)/cholesky | solution.py:110
  297.6 12.1 %cholesky.485 = f32[128,128]{1,0:T(8,128)S(1)} custom-call(f32[128,128]{1,0:T(8,128)S(1)} %cholesky.591), custom_call_target="Cholesky" | custom-call | tf_op jit(solution)/shard_map/jit(cholesky)/cholesky | solution.py:110
  310.4 9.8 %custom-call.65 = f32[1,128,128]{1,2,0:T(8,128)S(1)} custom-call(f32[1,128,128]{2,1,0:T(8,128)S(1)} %get-tuple-element.88), custom_call_target="InvertDiagBlocksLowerTriangular" | custom-call | tf_op jit(solution)/shard_map/jit(cholesky)/cholesky | solution.py:110
  323.7 11.7 %cholesky.504 = f32[128,128]{1,0:T(8,128)S(1)} custom-call(f32[128,128]{1,0:T(8,128)S(1)} %cholesky.596), custom_call_target="Cholesky" | custom-call | tf_op jit(solution)/shard_map/jit(cholesky)/cholesky | solution.py:110
  336.0 10.0 %custom-call.66 = f32[1,128,128]{1,2,0:T(8,128)S(1)} custom-call(f32[1,128,128]{2,1,0:T(8,128)S(1)} %get-tuple-element.85), custom_call_target="InvertDiagBlocksLowerTriangular" | custom-call | tf_op jit(solution)/shard_map/jit(cholesky)/cholesky | solution.py:110
  351.0 11.7 %cholesky.524 = f32[128,128]{1,0:T(8,128)S(1)} custom-call(f32[128,128]{1,0:T(8,128)S(1)} %cholesky.601), custom_call_target="Cholesky" | custom-call | tf_op jit(solution)/shard_map/jit(cholesky)/cholesky | solution.py:110
  363.4 9.8 %custom-call.67 = f32[1,128,128]{1,2,0:T(8,128)S(1)} custom-call(f32[1,128,128]{2,1,0:T(8,128)S(1)} %get-tuple-element.82), custom_call_target="InvertDiagBlocksLowerTriangular" | custom-call | tf_op jit(solution)/shard_map/jit(cholesky)/cholesky | solution.py:110
  376.2 12.1 %cholesky.544 = f32[128,128]{1,0:T(8,128)S(1)} custom-call(f32[128,128]{1,0:T(8,128)S(1)} %cholesky.606), custom_call_target="Cholesky" | custom-call | tf_op jit(solution)/shard_map/jit(cholesky)/cholesky | solution.py:110
  388.9 9.8 %custom-call.68 = f32[1,128,128]{1,2,0:T(8,128)S(1)} custom-call(f32[1,128,128]{2,1,0:T(8,128)S(1)} %get-tuple-element.79), custom_call_target="InvertDiagBlocksLowerTriangular" | custom-call | tf_op jit(solution)/shard_map/jit(cholesky)/cholesky | solution.py:110
  401.4 11.7 %cholesky.562 = f32[128,128]{1,0:T(8,128)S(1)} custom-call(f32[128,128]{1,0:T(8,128)S(1)} %convolution_subtract_fusion.12), custom_call_target="Cholesky" | custom-call | tf_op jit(solution)/shard_map/jit(cholesky)/cholesky | solution.py:110
  428.9 22.4 %while.3 = (s32[]{:T(128)}, f32[1024,1024]{1,0:T(8,128)}, s32[8,2]{0,1:T(2,128)S(1)}, f32[8,128,128]{2,1,0:T(8,128)S(1)}, s32[]{:T(128)}) while((s32[]{:T(128)}, f32[1024,1024]{1,0:T(8,128)}, s32[8,2]{0,1:T(2,128)S(1)}, f32[8,128,128]{2,1,0:T(8,128)S(1)}, s32[]{:T(128)}) %tuple.71), condition=%wide.while_cond.2, body=%wide.while_body.2.sunk | while | flops 2 | bytes 131189 | solution.py:111
  451.3 79.2 %custom-call.69 = f32[8,128,128]{1,2,0:T(8,128)} custom-call(f32[8,128,128]{2,1,0:T(8,128)S(1)} %get-tuple-element.40), custom_call_target="InvertDiagBlocksLowerTriangular" | custom-call | tf_op jit(solution)/shard_map/triangular_solve | solution.py:111
  543.0 5.7 fusion.103
  548.7 9.7 %select_add_fusion = f32[1280,1024]{1,0:T(8,128)S(1)} fusion(bf16[1024,2432]{1,0:T(8,128)(2,1)} %reshape.368, bf16[640,2432]{1,0:T(8,128)(2,1)S(1)} %copy-done.5, bf16[640,2432]{1,0:T(8,128)(2,1)S(1)} %copy-done.6, f32[1024]{0:T(1024)S(1)} %broadcast_in_dim.82, s32[1280]{0:T(1024)S(1)} %pad_add_fusion), kind=kOutput, calls=%fused_computation.6 | convolution fusion | flops 6391726080 | bytes 16458752 | tf_op jit(solution)/shard_map/dot_general | solution.py:101
  571.4 5.3 fusion.18
  577.5 7.0 %convolution_subtract_fusion = f32[1280,128]{1,0:T(8,128)S(1)} fusion(f32[1280,640]{0,1:T(8,128)S(1)} %get-tuple-element.59, f32[1280,1024]{1,0:T(8,128)S(1)} %select_add_fusion, f32[1024,1024]{1,0:T(8,128)} %get-tuple-element.160), kind=kOutput, calls=%fused_computation.28 | convolution fusion | flops 1258455040 | bytes 4915200 | tf_op jit(solution)/shard_map/triangular_solve | solution.py:111
  585.2 7.5 %convolution_subtract_fusion.1 = f32[1280,128]{1,0:T(8,128)S(1)} fusion(f32[1280,768]{0,1:T(8,128)S(1)} %get-tuple-element.55, f32[1280,1024]{1,0:T(8,128)S(1)} %select_add_fusion, f32[1024,1024]{1,0:T(8,128)} %get-tuple-element.160), kind=kOutput, calls=%fused_computation.30 | convolution fusion | flops 1510113280 | bytes 5636096 | tf_op jit(solution)/shard_map/triangular_solve | solution.py:111
  593.4 8.8 %convolution_subtract_fusion.5 = f32[1280,128]{1,0:T(8,128)S(1)} fusion(f32[1280,896]{0,1:T(8,128)S(1)} %get-tuple-element.51, f32[1280,1024]{1,0:T(8,128)S(1)} %select_add_fusion, f32[1024,1024]{1,0:T(8,128)} %get-tuple-element.160), kind=kOutput, calls=%fused_computation.34 | convolution fusion | flops 1761771520 | bytes 6356992 | tf_op jit(solution)/shard_map/triangular_solve | solution.py:111
  605.6 9.4 %fusion.27 = f32[640,576]{0,1:T(8,128)S(1)} fusion(f32[640,640]{0,1:T(8,128)S(1)} %fusion.103, f32[1280,1024]{0,1:T(8,128)} %copy-done.2, f32[576]{0:T(1024)S(1)} %slice.346, s32[640]{0:T(1024)S(1)} %add.222, s32[576]{0:T(1024)S(1)} %slice.345, pred[640]{0:T(1024)(128)(4,1)S(1)} %broadcast_compare_fusion), kind=kOutput, calls=%fused_computation.43 | convolution fusion | flops 4531691520 | bytes 8199808 | tf_op jit(solution)/shard_map/dot_general | solution.py:126
  (162 shorter events, 116.9 us)
Async XLA Ops:
  6.5 2.1 copy-start
  6.5 101.8 %all-gather.17.cloned.1.call-start = ((), (), s32[]{:S(2)}) async-start(), calls=%async_computation.3 | async-start | bytes 1984512 | tf_op jit(solution)/shard_map/all_gather | solution.py:60
  22.6 88.5 %copy-start.8 = (f32[40]{0:T(128)S(1)}, f32[40]{0:T(128)}, u32[]{:S(2)}) copy-start(f32[40]{0:T(128)} %param.11) | copy-start | bytes 484
  23.8 153.4 %copy-start.4 = (bf16[4,10,4,2432]{3,2,1,0:T(4,128)(2,1)}, bf16[4,10,4,2432]{3,2,1,0:T(4,128)(2,1)S(1)}, u32[]{:S(2)}) copy-start(bf16[4,10,4,2432]{3,2,1,0:T(4,128)(2,1)S(1)} %reshape.364) | copy-start | bytes 2334724
  25.6 145.8 %all-gather.13.cloned.1.call-start = ((), (), s32[]{:S(2)}) async-start(), calls=%async_computation.1 | async-start | bytes 6615040 | tf_op jit(solution)/shard_map/all_gather | solution.py:61
  111.0 419.5 %all-gather.15.cloned.1.call-start = ((), (), s32[]{:S(2)}) async-start(), calls=%async_computation.2 | async-start | bytes 3891200 | tf_op jit(solution)/shard_map/all_gather | solution.py:74
  177.2 359.5 %all-gather.11.cloned.1.call-start = ((), (), s32[]{:S(2)}) async-start(), calls=%async_computation | async-start | bytes 3307520 | tf_op jit(solution)/shard_map/all_gather | solution.py:71
  216.2 1.9 copy-start.3
  543.0 5.7 copy-start.5
  543.0 5.7 copy-start.6
  548.7 9.7 %copy-start.7 = (f32[8,128,128]{1,2,0:T(8,128)S(1)}, f32[8,128,128]{1,2,0:T(8,128)}, u32[]{:S(2)}) copy-start(f32[8,128,128]{1,2,0:T(8,128)} %custom-call.69) | copy-start | bytes 1572868
  602.9 2.3 copy-start.2
  605.6 11.3 %copy-start.1 = (bf16[2,304,160]{1,2,0:T(8,128)(2,1)S(1)}, bf16[2,304,160]{1,2,0:T(8,128)(2,1)}, u32[]{:S(2)}) copy-start(bf16[2,304,160]{1,2,0:T(8,128)(2,1)} %param.8) | copy-start | bytes 583684
Sparse Core Ops, SparseCore 0:
  25.7 82.5 all-gather.16
  111.1 60.2 all-gather.12
  177.3 42.4 all-gather.14
  347.8 90.5 all-gather.10

commit v3 on v2

--- a/solution.py
+++ b/solution.py
@@ -1,11 +1,75 @@
+import functools
+
 import jax
 import jax.numpy as jnp
 from jax import lax
+from jax.experimental import pallas as pl
+from jax.experimental.pallas import tpu as pltpu
 from jax.sharding import PartitionSpec as P
 
 PW = 1024
 PANELS = 1
 NPAN = 10
+HI = lax.Precision.HIGHEST
+
+
+def _base_inverse(s):
+    b = s.shape[0]
+    lane = lax.broadcasted_iota(jnp.int32, (b, b), 1)
+    sub = lax.broadcasted_iota(jnp.int32, (b, b), 0)
+    sub_col = lax.broadcasted_iota(jnp.int32, (b, 1), 0)
+    lane_row = lax.broadcasted_iota(jnp.int32, (1, b), 1)
+    eye = jnp.where(lane == sub, 1.0, 0.0).astype(jnp.float32)
+
+    def step(j, carry):
+        work, inv = carry
+        col = jnp.sum(jnp.where(lane == j, work, 0.0), axis=1, keepdims=True)
+        row = jnp.sum(jnp.where(sub == j, work, 0.0), axis=0, keepdims=True)
+        pivot = jnp.sum(jnp.where(lane_row == j, row, 0.0), axis=1, keepdims=True)
+        scale = lax.rsqrt(pivot)
+        l_col = jnp.where(sub_col >= j, col * scale, 0.0)
+        l_row = jnp.where(lane_row >= j, row * scale, 0.0)
+        work = work - l_col * l_row
+        inv_row = jnp.sum(jnp.where(sub == j, inv, 0.0), axis=0, keepdims=True)
+        diag = pivot * scale
+        u = jnp.where(sub_col == j, l_col - 1.0, l_col) / diag
+        inv = inv - u * inv_row
+        return work, inv
+
+    _, inv = lax.fori_loop(0, b, step, (s, eye))
+    return inv
+
+
+def _kernel(a_ref, z_ref, *, n, b):
+    z_ref[...] = jnp.zeros_like(z_ref)
+    for k in range(n // b):
+        lo = k * b
+        s = a_ref[lo:lo + b, lo:lo + b]
+        if k > 0:
+            zk = z_ref[0:lo, 0:lo]
+            left = lax.dot_general(a_ref[lo:lo + b, 0:lo], zk, (((1,), (1,)), ((), ())),
+                                   precision=HI, preferred_element_type=jnp.float32)
+            s = s - lax.dot_general(left, left, (((1,), (1,)), ((), ())),
+                                    precision=HI, preferred_element_type=jnp.float32)
+        d = _base_inverse(s)
+        z_ref[lo:lo + b, lo:lo + b] = d
+        if k > 0:
+            t = jnp.dot(left, zk, precision=HI, preferred_element_type=jnp.float32)
+            z_ref[lo:lo + b, 0:lo] = -jnp.dot(d, t, precision=HI, preferred_element_type=jnp.float32)
+
+
+def inverse_cholesky(a, b=128):
+    n = a.shape[0]
+    return pl.pallas_call(
+        functools.partial(_kernel, n=n, b=b),
+        out_shape=jax.ShapeDtypeStruct((n, n), jnp.float32),
+        in_specs=[pl.BlockSpec(memory_space=pltpu.VMEM)],
+        out_specs=pl.BlockSpec(memory_space=pltpu.VMEM),
+        compiler_params=pltpu.CompilerParams(vmem_limit_bytes=48 * 1024 * 1024),
+        cost_estimate=pl.CostEstimate(
+            flops=2 * n * n * n, transcendentals=n, bytes_accessed=8 * n * n
+        ),
+    )(a)
 
 
 def split3(x):
@@ -107,9 +171,9 @@
         row_global[:, None] == col_global[None, :], shift_col[None, :], 0.0
     )
 
-    cholesky_factor = jnp.linalg.cholesky(diag_block)
-    solved = lax.linalg.triangular_solve(
-        cholesky_factor, both_panel, left_side=False, lower=True, transpose_a=True
+    inverse_factor_panel = inverse_cholesky(diag_block)
+    solved = lax.dot_general(
+        both_panel, inverse_factor_panel, dims, precision=highest, preferred_element_type=f32
     )
     local_rows = row_global.shape[0]
     row_factor = solved[:local_rows]

time: 633 us -> 444 us (0.70)
  other arithmetic: 267 us -> 5.46 us
  Pallas kernels: 0 us -> 159 us
  matrix products: 105 us -> 57.6 us
  local copies, waits for them, and re-layouts: 78.8 us -> 47 us
    another operation x37 -> x3, other arithmetic: 259 us -> 2.11 us  [the longest x31 173 us: local(): cholesky_factor = jnp.linalg.cholesky(diag_block)]
    pallas_call x0 -> x1, Pallas kernels: none -> 159 us  [inverse_cholesky(): pl.pallas_call(functools.partial(_kernel, n=n, b=b), out_shape=jax.ShapeD...]
    another operation x29 -> x0, matrix products: 67.6 us -> none  [the longest x15 44.5 us: local(): lax.linalg.triangular_solve(cholesky_factor, both_panel, left_side=False,...]
    another operation x33 -> x0, local copies, waits for them, and re-layouts: 24.8 us -> none
    dot_general x0 -> x1, matrix products: none -> 18.5 us  [local(): lax.dot_general(both_panel, inverse_factor_panel, dims, precision=highest...]
  transfers between devices with their start and end apart: 4 -> 4, of which waited for: 2 -> 2; matrix products, arithmetic and copies ran while one was open for 57% -> 9% of each run, Pallas kernels for 0% -> 36%
where the time goes in v3:
time: 444 us; the launch traced here: 437 us
  Pallas kernels  159 us (36%)
  waiting for transfers between devices  143 us (32%)
  matrix products  57.6 us (13%)
  local copies, waits for them, and re-layouts  47 us (11%)
  between operations  13.8 us (3%)
  blocking collectives  10.5 us (2%)
  other arithmetic  5.46 us (1%)
    pallas_call x1, Pallas kernels, inverse_cholesky(): pl.pallas_call(functools.partial(_kernel, n=n, b=b), out_shape=jax.ShapeD...  159 us
    all_gather x1, waiting for transfers between devices, local(): panel_w = lax.all_gather(panel_w, 'col', axis=0, tiled=False)  82.6 us
    all_gather x1, waiting for transfers between devices, local(): panel_w = lax.all_gather(panel_w, 'row', axis=0, tiled=False)  60.4 us
    dot_general x1, matrix products, local(): lax.dot_general(both_panel, inverse_factor_panel, dims, precision=highest...  18.5 us
    dot_general x1, matrix products, local(): lax.dot_general(panel_w, panel_w, dims, preferred_element_type=f32)  11 us
    all_gather x1, blocking collectives, local(): lax.all_gather(jnp.concatenate([whitened, shift_row], axis=0), 'grp', axi...  10.5 us
    dot_general x1, matrix products, local(): lax.dot_general(both_w, panel_w, dims, preferred_element_type=f32)  10.5 us
    reshape x1, local copies, waits for them, and re-layouts, local(): panel_w = jnp.transpose(panel_w, (2, 0, 1, 3, 4)).reshape(PW, total)  9.03 us
  transfers between devices with their start and end apart: 4, of which 2 were waited for; matrix products, arithmetic and copies ran while one was open for 9% of the time, Pallas kernels for 36%

profile of v3, /device:TPU:1, one launch (start us, length us, event | category | flops | bytes accessed | tf_op | source)
XLA Modules:
  0.0 436.7 jit_solution(254358300479632762)
XLA Ops:
  6.5 0.7 compare_reduce_fusion
  7.2 0.7 fusion.29
  7.9 0.7 compare_convert_fusion
  8.6 2.1 fusion.16
  11.1 0.7 broadcast_select_fusion.1
  11.8 10.5 %all-gather.4 = bf16[4,161,608]{2,1,0:T(8,128)(2,1)S(1)} all-gather(bf16[1,161,608]{2,1,0:T(8,128)(2,1)S(1)} %fusion.24), channel_id=2, replica_groups=mesh['grp'=4,'row'=4,'col'=16] {'grp'}, dimensions={0}, use_global_device_ids=true | all-gather | bytes 978880 | tf_op jit(solution)/shard_map/all_gather | solution.py:114
  22.9 0.8 reshape.297
  24.1 0.7 broadcast_select_fusion
  24.8 0.7 fusion.26
  25.6 82.6 %all-gather.17.cloned.1.call-done = bf16[16,17,2432]{2,1,0:T(8,128)(2,1)} async-done(((bf16[1,17,2432]{2,1,0:T(8,128)(2,1)}), bf16[16,17,2432]{2,1,0:T(8,128)(2,1)}) %all-gather.17.cloned.1.call-update) | async-done | bytes 1323024 | tf_op jit(solution)/shard_map/all_gather | solution.py:124
  108.2 2.7 copy.19
  111.0 60.4 %all-gather.13.cloned.1.call-done = bf16[64,17,2432]{2,0,1:T(8,128)(2,1)} async-done(((bf16[16,17,2432]{2,0,1:T(8,128)(2,1)}), bf16[64,17,2432]{2,0,1:T(8,128)(2,1)}) %all-gather.13.cloned.1.call-update) | async-done | bytes 5292048 | tf_op jit(solution)/shard_map/all_gather | solution.py:125
  171.4 1.7 constant_dynamic-slice_fusion.1
  174.0 2.8 slice.91
  176.8 6.1 %copy.29 = bf16[4,16,4,4,2432]{4,3,1,0,2:T(4,128)(2,1)} copy(bf16[4,16,4,4,2432]{4,1,0,3,2:T(8,128)(2,1)S(1)} %bitcast.50) | data formatting | bytes 9961472 | tf_op jit(solution)/shard_map/reshape | solution.py:131
  182.9 9.0 %reshape.301 = bf16[1024,2432]{1,0:T(8,128)(2,1)} reshape(bf16[4,4,16,4,2432]{4,3,2,1,0:T(4,128)(2,1)} %bitcast.49) | data formatting | bytes 9961472 | tf_op jit(solution)/shard_map/reshape | solution.py:132
  191.9 0.7 slice_convert_fusion
  193.2 11.0 %select_add_fusion.a_ref = f32[1024,1024]{1,0:T(8,128)} fusion(f32[1024]{0:T(1024)S(1)} %broadcast_in_dim.78, bf16[1024,2432]{1,0:T(8,128)(2,1)} %reshape.301), kind=kOutput, calls=%fused_computation.9 | convolution fusion | flops 5103419392 | bytes 9179136 | tf_op jit(solution)/shard_map/dot_general | solution.py:159
  204.2 159.1 %shard_map.46 = f32[1024,1024]{1,0:T(8,128)S(1)} custom-call(f32[1024,1024]{1,0:T(8,128)} %select_add_fusion.a_ref), custom_call_target="tpu_custom_call" | custom-call | flops 2147483648 | bytes 8388608 | tf_op jit(solution)/shard_map/pallas_call | solution.py:63
  363.3 1.9 copy-done.2
  365.2 3.1 copy.30
  368.4 3.2 reshape.299
  371.6 3.1 copy.20
  374.7 2.9 reshape.298
  377.7 6.8 %fusion.40 = f32[640,640]{0,1:T(8,128)} fusion(bf16[640,2432]{1,0:T(8,128)(2,1)} %reshape.298, bf16[640,2432]{1,0:T(8,128)(2,1)} %reshape.299), kind=kOutput, calls=%fused_computation.79 | convolution fusion | flops 1992294400 | bytes 7864320 | tf_op jit(solution)/shard_map/dot_general | solution.py:169
  384.5 10.5 %fusion = f32[1280,1024]{1,0:T(8,128)S(1)} fusion(bf16[1024,2432]{1,0:T(8,128)(2,1)} %reshape.301, bf16[640,2432]{1,0:T(8,128)(2,1)S(1)} %copy-done.6, bf16[640,2432]{1,0:T(8,128)(2,1)S(1)} %copy-done.7), kind=kOutput, calls=%fused_computation | convolution fusion | flops 6387793920 | bytes 16449536 | tf_op jit(solution)/shard_map/dot_general | solution.py:165
  395.0 18.5 %fusion.4 = f32[1280,1024]{1,0:T(8,128)S(1)} fusion(f32[1024,1024]{1,0:T(8,128)S(1)} %copy-done.3, f32[1280,1024]{1,0:T(8,128)S(1)} %fusion, f32[1024]{0:T(1024)S(1)} %broadcast_in_dim.78, s32[1280]{0:T(1024)S(1)} %pad_add_fusion), kind=kOutput, calls=%fused_computation.4 | convolution fusion | flops 16110059520 | bytes 14689280 | tf_op jit(solution)/shard_map/dot_general | solution.py:175
  413.5 2.3 copy-done.4
  416.0 2.1 copy.25
  418.0 1.0 constant_dynamic-slice_fusion
  419.2 8.8 %fusion.13 = f32[640,576]{0,1:T(8,128)S(1)} fusion(f32[640,640]{0,1:T(8,128)} %fusion.40, f32[1280,1024]{1,0:T(8,128)} %copy-done.4, f32[576]{0:T(1024)S(1)} %slice.112, s32[640]{0:T(1024)S(1)} %add.143, s32[576]{0:T(1024)S(1)} %slice.111, pred[640]{0:T(1024)(128)(4,1)S(1)} %broadcast_compare_fusion), kind=kOutput, calls=%fused_computation.20 | convolution fusion | flops 4531691520 | bytes 7937664 | tf_op jit(solution)/shard_map/dot_general | solution.py:190
  428.1 1.7 copy.26
  (65 shorter events, 3.3 us)
Async XLA Ops:
  6.5 2.1 copy-start
  6.5 101.6 %all-gather.17.cloned.1.call-start = ((), (), s32[]{:S(2)}) async-start(), calls=%async_computation.3 | async-start | bytes 1984512 | tf_op jit(solution)/shard_map/all_gather | solution.py:124
  22.9 150.2 %copy-start.8 = (f32[40]{0:T(128)S(1)}, f32[40]{0:T(128)}, u32[]{:S(2)}) copy-start(f32[40]{0:T(128)} %param.11) | copy-start | bytes 484
  23.7 147.6 %copy-start.5 = (bf16[4,10,4,2432]{3,2,1,0:T(4,128)(2,1)}, bf16[4,10,4,2432]{3,2,1,0:T(4,128)(2,1)S(1)}, u32[]{:S(2)}) copy-start(bf16[4,10,4,2432]{3,2,1,0:T(4,128)(2,1)S(1)} %reshape.297) | copy-start | bytes 2334724
  25.5 145.8 %all-gather.13.cloned.1.call-start = ((), (), s32[]{:S(2)}) async-start(), calls=%async_computation.1 | async-start | bytes 6615040 | tf_op jit(solution)/shard_map/all_gather | solution.py:125
  110.9 254.3 %all-gather.15.cloned.1.call-start = ((), (), s32[]{:S(2)}) async-start(), calls=%async_computation.2 | async-start | bytes 3891200 | tf_op jit(solution)/shard_map/all_gather | solution.py:138
  171.3 200.2 %all-gather.11.cloned.1.call-start = ((), (), s32[]{:S(2)}) async-start(), calls=%async_computation | async-start | bytes 3307520 | tf_op jit(solution)/shard_map/all_gather | solution.py:135
  363.3 1.9 copy-start.2
  377.7 6.8 %copy-start.6 = (bf16[640,2432]{1,0:T(8,128)(2,1)S(1)}, bf16[640,2432]{1,0:T(8,128)(2,1)}, u32[]{:S(2)}) copy-start(bf16[640,2432]{1,0:T(8,128)(2,1)} %reshape.299) | copy-start | bytes 9338884
  377.7 6.8 %copy-start.7 = (bf16[640,2432]{1,0:T(8,128)(2,1)S(1)}, bf16[640,2432]{1,0:T(8,128)(2,1)}, u32[]{:S(2)}) copy-start(bf16[640,2432]{1,0:T(8,128)(2,1)} %reshape.298) | copy-start | bytes 9338884
  384.5 10.5 %copy-start.3 = (f32[1024,1024]{1,0:T(8,128)S(1)}, f32[1024,1024]{1,0:T(8,128)}, u32[]{:S(2)}) copy-start(f32[1024,1024]{1,0:T(8,128)} %copy-done.2) | copy-start | bytes 12582916
  413.5 2.3 copy-start.4
  419.2 10.6 %copy-start.1 = (bf16[2,304,160]{1,2,0:T(8,128)(2,1)S(1)}, bf16[2,304,160]{1,2,0:T(8,128)(2,1)}, u32[]{:S(2)}) copy-start(bf16[2,304,160]{1,2,0:T(8,128)(2,1)} %param.8) | copy-start | bytes 583684
Sparse Core Ops, SparseCore 0:
  25.6 82.5 all-gather.16
  111.0 60.2 all-gather.12
  173.1 42.3 all-gather.14
  218.0 89.8 all-gather.10

commit v4 on v3

--- a/solution.py
+++ b/solution.py
@@ -121,7 +121,9 @@
         split3(shift_grp[:, 0].reshape(-1))
     )
     panel_w = jnp.concatenate([every[:, 0].reshape(groups * window, total), panel_shift_row], 0)
-    panel_w = lax.all_gather(panel_w, "col", axis=0, tiled=False)
+    panel_w = lax.all_to_all(
+        jnp.broadcast_to(panel_w[None], (colcount,) + panel_w.shape), "col", 0, 0, tiled=False
+    )
     panel_w = lax.all_gather(panel_w, "row", axis=0, tiled=False)
     every, panel_w = lax.optimization_barrier((every, panel_w))
     shift_panel = join3(panel_w[:, :, groups * window, : 3 * groups * window])

time: 444 us -> 412 us (0.928)
  waiting for transfers between devices: 143 us -> 55.7 us
  blocking collectives: 10.5 us -> 67.7 us
    all_gather x1 -> x0, waiting for transfers between devices: 82.6 us -> none  [local(): panel_w = lax.all_gather(panel_w, 'col', axis=0, tiled=False)]
    all_to_all x0 -> x1, blocking collectives: none -> 57.2 us  [local(): lax.all_to_all(jnp.broadcast_to(panel_w[None], (colcount,) + panel_w.shap...]
    transpose x0 -> x1, local copies, waits for them, and re-layouts: none -> 6.15 us  [local(): panel_w = jnp.transpose(panel_w, (2, 0, 1, 3, 4)).reshape(PW, total)]
    reshape x1 -> x0, local copies, waits for them, and re-layouts: 6.14 us -> none  [local(): panel_w[:, :, :groups * window]]
    all_gather x1, waiting for transfers between devices: 60.4 us -> 55.7 us  [local(): panel_w = lax.all_gather(panel_w, 'row', axis=0, tiled=False)]
  transfers between devices with their start and end apart: 4 -> 3, of which waited for: 2 -> 1; matrix products, arithmetic and copies ran while one was open for 9% -> 10% of each run, Pallas kernels for 36% -> 39%
where the time goes in v4:
time: 412 us; the launch traced here: 405 us
  Pallas kernels  159 us (39%)
  blocking collectives  67.7 us (16%)
  matrix products  57.6 us (14%)
  waiting for transfers between devices  55.7 us (14%)
  local copies, waits for them, and re-layouts  45.7 us (11%)
  between operations  13.8 us (3%)
  other arithmetic  4.91 us (1%)
    pallas_call x1, Pallas kernels, inverse_cholesky(): pl.pallas_call(functools.partial(_kernel, n=n, b=b), out_shape=jax.ShapeD...  159 us
    all_to_all x1, blocking collectives, local(): lax.all_to_all(jnp.broadcast_to(panel_w[None], (colcount,) + panel_w.shap...  57.2 us
    all_gather x1, waiting for transfers between devices, local(): panel_w = lax.all_gather(panel_w, 'row', axis=0, tiled=False)  55.7 us
    dot_general x1, matrix products, local(): lax.dot_general(both_panel, inverse_factor_panel, dims, precision=highest...  18.5 us
    dot_general x1, matrix products, local(): lax.dot_general(panel_w, panel_w, dims, preferred_element_type=f32)  10.9 us
    all_gather x1, blocking collectives, local(): lax.all_gather(jnp.concatenate([whitened, shift_row], axis=0), 'grp', axi...  10.5 us
    dot_general x1, matrix products, local(): lax.dot_general(both_w, panel_w, dims, preferred_element_type=f32)  10.5 us
    reshape x1, local copies, waits for them, and re-layouts, local(): panel_w = jnp.transpose(panel_w, (2, 0, 1, 3, 4)).reshape(PW, total)  9.04 us
  transfers between devices with their start and end apart: 3, of which 1 were waited for; matrix products, arithmetic and copies ran while one was open for 10% of the time, Pallas kernels for 39%

profile of v4, /device:TPU:1, one launch (start us, length us, event | category | flops | bytes accessed | tf_op | source)
XLA Modules:
  0.0 404.7 jit_solution(18151382504988091)
XLA Ops:
  6.5 0.7 compare_reduce_fusion
  7.3 0.7 fusion.28
  7.9 0.7 compare_convert_fusion
  8.6 2.1 fusion.16
  11.1 0.8 broadcast_select_fusion.1
  11.9 10.5 %all-gather.3 = bf16[4,161,608]{2,1,0:T(8,128)(2,1)S(1)} all-gather(bf16[1,161,608]{2,1,0:T(8,128)(2,1)S(1)} %fusion.24), channel_id=2, replica_groups=mesh['grp'=4,'row'=4,'col'=16] {'grp'}, dimensions={0}, use_global_device_ids=true | all-gather | bytes 978880 | tf_op jit(solution)/shard_map/all_gather | solution.py:114
  22.6 0.4 copy.35
  23.0 0.8 reshape.298
  24.2 0.7 broadcast_select_fusion
  25.1 57.2 %all_to_all.5 = bf16[16,17,2432]{2,1,0:T(8,128)(2,1)S(1)} all-to-all(bf16[16,17,2432]{2,1,0:T(8,128)(2,1)S(1)} %broadcast_in_dim.84), channel_id=1, replica_groups=mesh['grp'=4,'row'=4,'col'=16] {'col'}, dimensions={0} | all-to-all | bytes 2646016 | tf_op jit(solution)/shard_map/all_to_all | solution.py:124
  82.3 1.2 copy.36
  83.5 55.7 %all-gather.10.cloned.1.call-done = bf16[64,17,2432]{2,0,1:T(8,128)(2,1)} async-done(((bf16[16,17,2432]{2,0,1:T(8,128)(2,1)}), bf16[64,17,2432]{2,0,1:T(8,128)(2,1)}) %all-gather.10.cloned.1.call-update) | async-done | bytes 5292048 | tf_op jit(solution)/shard_map/all_gather | solution.py:127
  139.3 1.7 constant_dynamic-slice_fusion.1
  141.9 2.8 slice.91
  144.7 6.2 %copy.40 = bf16[4,4,16,4,2432]{4,3,2,1,0:T(4,128)(2,1)} copy(bf16[4,4,16,4,2432]{4,2,1,3,0:T(8,128)(2,1)S(1)} %bitcast.46) | data formatting | bytes 9961472 | tf_op jit(solution)/shard_map/transpose | solution.py:134
  150.8 9.0 %reshape.302 = bf16[1024,2432]{1,0:T(8,128)(2,1)} reshape(bf16[4,4,16,4,2432]{4,3,2,1,0:T(4,128)(2,1)} %copy.40) | data formatting | bytes 9961472 | tf_op jit(solution)/shard_map/reshape | solution.py:134
  159.9 0.7 slice_convert_fusion
  161.1 10.9 %select_add_fusion.a_ref = f32[1024,1024]{1,0:T(8,128)} fusion(f32[1024]{0:T(1024)S(1)} %broadcast_in_dim.85, bf16[1024,2432]{1,0:T(8,128)(2,1)} %reshape.302), kind=kOutput, calls=%fused_computation.8 | convolution fusion | flops 5103419392 | bytes 9179136 | tf_op jit(solution)/shard_map/dot_general | solution.py:161
  172.1 159.1 %shard_map.46 = f32[1024,1024]{1,0:T(8,128)S(1)} custom-call(f32[1024,1024]{1,0:T(8,128)} %select_add_fusion.a_ref), custom_call_target="tpu_custom_call" | custom-call | flops 2147483648 | bytes 8388608 | tf_op jit(solution)/shard_map/pallas_call | solution.py:63
  331.2 1.9 copy-done.2
  333.1 3.1 copy.47
  336.3 3.2 reshape.300
  339.5 3.1 copy.37
  342.6 3.0 reshape.299
  345.6 6.8 %fusion.39 = f32[640,640]{0,1:T(8,128)} fusion(bf16[640,2432]{1,0:T(8,128)(2,1)} %reshape.299, bf16[640,2432]{1,0:T(8,128)(2,1)} %reshape.300), kind=kOutput, calls=%fused_computation.77 | convolution fusion | flops 1992294400 | bytes 7864320 | tf_op jit(solution)/shard_map/dot_general | solution.py:171
  352.4 10.5 %fusion = f32[1280,1024]{1,0:T(8,128)S(1)} fusion(bf16[1024,2432]{1,0:T(8,128)(2,1)} %reshape.302, bf16[640,2432]{1,0:T(8,128)(2,1)S(1)} %copy-done.6, bf16[640,2432]{1,0:T(8,128)(2,1)S(1)} %copy-done.7), kind=kOutput, calls=%fused_computation | convolution fusion | flops 6387793920 | bytes 16449536 | tf_op jit(solution)/shard_map/dot_general | solution.py:167
  362.9 18.5 %fusion.4 = f32[1280,1024]{1,0:T(8,128)S(1)} fusion(f32[1024,1024]{1,0:T(8,128)S(1)} %copy-done.3, f32[1280,1024]{1,0:T(8,128)S(1)} %fusion, f32[1024]{0:T(1024)S(1)} %broadcast_in_dim.85, s32[1280]{0:T(1024)S(1)} %pad_add_fusion), kind=kOutput, calls=%fused_computation.4 | convolution fusion | flops 16110059520 | bytes 14689280 | tf_op jit(solution)/shard_map/dot_general | solution.py:177
  381.4 2.3 copy-done.4
  383.9 2.1 copy.43
  386.0 1.0 constant_dynamic-slice_fusion
  387.2 8.8 %fusion.13 = f32[640,576]{0,1:T(8,128)S(1)} fusion(f32[640,640]{0,1:T(8,128)} %fusion.39, f32[1280,1024]{1,0:T(8,128)} %copy-done.4, f32[576]{0:T(1024)S(1)} %slice.112, s32[640]{0:T(1024)S(1)} %add.143, s32[576]{0:T(1024)S(1)} %slice.111, pred[640]{0:T(1024)(128)(4,1)S(1)} %broadcast_compare_fusion), kind=kOutput, calls=%fused_computation.19 | convolution fusion | flops 4531691520 | bytes 7937664 | tf_op jit(solution)/shard_map/dot_general | solution.py:192
  396.1 1.7 copy.44
  (64 shorter events, 3.0 us)
Async XLA Ops:
  6.5 2.1 copy-start
  6.5 132.7 %all-gather.10.cloned.1.call-start = ((), (), s32[]{:S(2)}) async-start(), calls=%async_computation.2 | async-start | bytes 6615040 | tf_op jit(solution)/shard_map/all_gather | solution.py:127
  23.8 59.7 %copy-start.5 = (bf16[4,10,4,2432]{3,2,1,0:T(4,128)(2,1)}, bf16[4,10,4,2432]{3,2,1,0:T(4,128)(2,1)S(1)}, u32[]{:S(2)}) copy-start(bf16[4,10,4,2432]{3,2,1,0:T(4,128)(2,1)S(1)} %reshape.298) | copy-start | bytes 2334724
  25.0 115.9 %copy-start.8 = (f32[40]{0:T(128)S(1)}, f32[40]{0:T(128)}, u32[]{:S(2)}) copy-start(f32[40]{0:T(128)} %param.11) | copy-start | bytes 484
  83.5 249.6 %all-gather.12.cloned.1.call-start = ((), (), s32[]{:S(2)}) async-start(), calls=%async_computation.3 | async-start | bytes 3891200 | tf_op jit(solution)/shard_map/all_gather | solution.py:140
  139.2 200.3 %all-gather.8.cloned.1.call-start = ((), (), s32[]{:S(2)}) async-start(), calls=%async_computation.1 | async-start | bytes 3307520 | tf_op jit(solution)/shard_map/all_gather | solution.py:137
  331.2 1.9 copy-start.2
  345.6 6.8 %copy-start.6 = (bf16[640,2432]{1,0:T(8,128)(2,1)S(1)}, bf16[640,2432]{1,0:T(8,128)(2,1)}, u32[]{:S(2)}) copy-start(bf16[640,2432]{1,0:T(8,128)(2,1)} %reshape.300) | copy-start | bytes 9338884
  345.6 6.8 %copy-start.7 = (bf16[640,2432]{1,0:T(8,128)(2,1)S(1)}, bf16[640,2432]{1,0:T(8,128)(2,1)}, u32[]{:S(2)}) copy-start(bf16[640,2432]{1,0:T(8,128)(2,1)} %reshape.299) | copy-start | bytes 9338884
  352.4 10.5 %copy-start.3 = (f32[1024,1024]{1,0:T(8,128)S(1)}, f32[1024,1024]{1,0:T(8,128)}, u32[]{:S(2)}) copy-start(f32[1024,1024]{1,0:T(8,128)} %copy-done.2) | copy-start | bytes 12582916
  381.4 2.3 copy-start.4
  387.2 10.6 %copy-start.1 = (bf16[2,304,160]{1,2,0:T(8,128)(2,1)S(1)}, bf16[2,304,160]{1,2,0:T(8,128)(2,1)}, u32[]{:S(2)}) copy-start(bf16[2,304,160]{1,2,0:T(8,128)(2,1)} %param.8) | copy-start | bytes 583684
Sparse Core Ops, SparseCore 0:
  83.6 55.5 all-gather.9
  141.0 42.3 all-gather.11
  186.1 89.7 all-gather.7

commit v5 on v4

--- a/solution.py
+++ b/solution.py
@@ -87,6 +87,7 @@
 
 def local(block_rows, inverse_factor, live_rows, shift):
     highest = lax.Precision.HIGHEST
+    high = lax.Precision.HIGH
     groups = lax.axis_size("grp")
     rowcount = lax.axis_size("row")
     colcount = lax.axis_size("col")
@@ -122,9 +123,12 @@
     )
     panel_w = jnp.concatenate([every[:, 0].reshape(groups * window, total), panel_shift_row], 0)
     panel_w = lax.all_to_all(
-        jnp.broadcast_to(panel_w[None], (colcount,) + panel_w.shape), "col", 0, 0, tiled=False
-    )
-    panel_w = lax.all_gather(panel_w, "row", axis=0, tiled=False)
+        jnp.broadcast_to(panel_w[None], (rowcount * colcount,) + panel_w.shape),
+        ("row", "col"),
+        0,
+        0,
+        tiled=False,
+    ).reshape((rowcount, colcount) + panel_w.shape)
     every, panel_w = lax.optimization_barrier((every, panel_w))
     shift_panel = join3(panel_w[:, :, groups * window, : 3 * groups * window])
     shift_panel = jnp.transpose(
@@ -175,7 +179,7 @@
 
     inverse_factor_panel = inverse_cholesky(diag_block)
     solved = lax.dot_general(
-        both_panel, inverse_factor_panel, dims, precision=highest, preferred_element_type=f32
+        both_panel, inverse_factor_panel, dims, precision=high, preferred_element_type=f32
     )
     local_rows = row_global.shape[0]
     row_factor = solved[:local_rows]
@@ -190,7 +194,7 @@
     boundary = PANELS * PW
     first_trailing = owners * window
     update = jnp.dot(
-        row_factor, col_factor[first_trailing:].T, precision=highest, preferred_element_type=f32
+        row_factor, col_factor[first_trailing:].T, precision=high, preferred_element_type=f32
     )
     trailing = schur_tile[:, first_trailing:] - update
     trailing = jnp.where(row_global[:, None] >= boundary, trailing, 0.0)

time: 412 us -> 470 us (1.14)
  blocking collectives: 67.7 us -> 191 us
  waiting for transfers between devices: 55.7 us -> 0.06 us
  matrix products: 57.6 us -> 45.2 us
    all_to_all x1, blocking collectives: 57.2 us -> 180 us  [local(): lax.all_to_all(jnp.broadcast_to(panel_w[None], (rowcount * colcount,) + p...]
    all_gather x1 -> x0, waiting for transfers between devices: 55.7 us -> none  [local(): panel_w = lax.all_gather(panel_w, 'row', axis=0, tiled=False)]
    dot_general x2, matrix products: 27.2 us -> 14.8 us  [the longest x1 8.88 us: local(): lax.dot_general(both_panel, inverse_factor_panel, dims, precision=high, p...]
  transfers between devices with their start and end apart: 3 -> 2, of which waited for: 1 -> 0; matrix products, arithmetic and copies ran while one was open for 10% -> 8% of each run, Pallas kernels for 39% -> 34%
where the time goes in v5:
time: 470 us; the launch traced here: 462 us
  blocking collectives  191 us (41%)
  Pallas kernels  159 us (34%)
  local copies, waits for them, and re-layouts  47.8 us (10%)
  matrix products  45.2 us (10%)
  between operations  13.9 us (3%)
  other arithmetic  4.78 us (1%)
    all_to_all x1, blocking collectives, local(): lax.all_to_all(jnp.broadcast_to(panel_w[None], (rowcount * colcount,) + p...  180 us
    pallas_call x1, Pallas kernels, inverse_cholesky(): pl.pallas_call(functools.partial(_kernel, n=n, b=b), out_shape=jax.ShapeD...  159 us
    dot_general x1, matrix products, local(): lax.dot_general(panel_w, panel_w, dims, preferred_element_type=f32)  11 us
    all_gather x1, blocking collectives, local(): lax.all_gather(jnp.concatenate([whitened, shift_row], axis=0), 'grp', axi...  10.5 us
    dot_general x1, matrix products, local(): lax.dot_general(both_w, panel_w, dims, preferred_element_type=f32)  10.5 us
  transfers between devices with their start and end apart: 2, of which 0 were waited for; matrix products, arithmetic and copies ran while one was open for 8% of the time, Pallas kernels for 34%

profile of v5, /device:TPU:1, one launch (start us, length us, event | category | flops | bytes accessed | tf_op | source)
XLA Modules:
  0.0 461.7 jit_solution(10012015912507326254)
XLA Ops:
  6.5 0.7 compare_reduce_fusion
  7.2 0.7 fusion.28
  7.9 0.7 compare_convert_fusion
  8.6 2.1 fusion.16
  11.1 0.7 broadcast_select_fusion.1
  11.8 10.5 %all-gather.2 = bf16[4,161,608]{2,1,0:T(8,128)(2,1)S(1)} all-gather(bf16[1,161,608]{2,1,0:T(8,128)(2,1)S(1)} %fusion.24), channel_id=2, replica_groups=mesh['grp'=4,'row'=4,'col'=16] {'grp'}, dimensions={0}, use_global_device_ids=true | all-gather | bytes 978880 | tf_op jit(solution)/shard_map/all_gather | solution.py:115
  22.5 0.4 copy.35
  22.9 0.8 reshape.301
  24.1 0.7 broadcast_select_fusion
  24.8 0.5 broadcast_in_dim.84
  25.3 180.4 %all_to_all.5 = bf16[64,17,2432]{2,1,0:T(8,128)(2,1)S(1)} all-to-all(bf16[64,17,2432]{2,1,0:T(8,128)(2,1)S(1)} %broadcast_in_dim.84), channel_id=1, replica_groups=mesh['grp'=4,'row'=4,'col'=16] {'row','col'}, dimensions={0} | all-to-all | bytes 10584064 | tf_op jit(solution)/shard_map/all_to_all | solution.py:125
  205.7 3.1 copy.36
  208.9 1.7 constant_dynamic-slice_fusion.1
  211.5 2.8 slice.91
  214.3 6.2 %copy.40 = bf16[4,4,16,4,2432]{4,3,2,1,0:T(4,128)(2,1)} copy(bf16[4,4,16,4,2432]{4,2,1,3,0:T(8,128)(2,1)S(1)} %bitcast.48) | data formatting | bytes 9961472 | tf_op jit(solution)/shard_map/transpose | solution.py:138
  220.4 8.9 %reshape.306 = bf16[1024,2432]{1,0:T(8,128)(2,1)} reshape(bf16[4,4,16,4,2432]{4,3,2,1,0:T(4,128)(2,1)} %copy.40) | data formatting | bytes 9961472 | tf_op jit(solution)/shard_map/reshape | solution.py:138
  229.3 0.7 slice_convert_fusion
  230.6 11.0 %select_add_fusion.a_ref = f32[1024,1024]{1,0:T(8,128)} fusion(f32[1024]{0:T(1024)S(1)} %broadcast_in_dim.85, bf16[1024,2432]{1,0:T(8,128)(2,1)} %reshape.306), kind=kOutput, calls=%fused_computation.8 | convolution fusion | flops 5103419392 | bytes 9179136 | tf_op jit(solution)/shard_map/dot_general | solution.py:165
  241.6 159.0 %shard_map.46 = f32[1024,1024]{1,0:T(8,128)S(1)} custom-call(f32[1024,1024]{1,0:T(8,128)} %select_add_fusion.a_ref), custom_call_target="tpu_custom_call" | custom-call | flops 2147483648 | bytes 8388608 | tf_op jit(solution)/shard_map/pallas_call | solution.py:63
  400.6 1.9 copy-done.2
  402.5 3.1 copy.47
  405.7 3.1 reshape.304
  408.9 3.1 copy.37
  412.0 3.0 reshape.303
  415.0 6.8 %fusion.39 = f32[640,640]{0,1:T(8,128)} fusion(bf16[640,2432]{1,0:T(8,128)(2,1)} %reshape.303, bf16[640,2432]{1,0:T(8,128)(2,1)} %reshape.304), kind=kOutput, calls=%fused_computation.77 | convolution fusion | flops 1992294400 | bytes 7864320 | tf_op jit(solution)/shard_map/dot_general | solution.py:175
  421.8 10.5 %fusion = f32[1280,1024]{1,0:T(8,128)S(1)} fusion(bf16[1024,2432]{1,0:T(8,128)(2,1)} %reshape.306, bf16[640,2432]{1,0:T(8,128)(2,1)S(1)} %copy-done.6, bf16[640,2432]{1,0:T(8,128)(2,1)S(1)} %copy-done.7), kind=kOutput, calls=%fused_computation | convolution fusion | flops 6387793920 | bytes 16449536 | tf_op jit(solution)/shard_map/dot_general | solution.py:171
  432.3 8.9 %fusion.4 = f32[1280,1024]{1,0:T(8,128)S(1)} fusion(f32[1024,1024]{1,0:T(8,128)S(1)} %copy-done.3, f32[1280,1024]{1,0:T(8,128)S(1)} %fusion, f32[1024]{0:T(1024)S(1)} %broadcast_in_dim.85, s32[1280]{0:T(1024)S(1)} %pad_add_fusion), kind=kOutput, calls=%fused_computation.4 | convolution fusion | flops 8056995840 | bytes 14689280 | tf_op jit(solution)/shard_map/dot_general | solution.py:181
  441.2 2.3 copy-done.4
  443.7 2.1 copy.43
  445.8 1.0 constant_dynamic-slice_fusion
  447.0 5.9 %fusion.13 = f32[640,576]{0,1:T(8,128)S(1)} fusion(f32[640,640]{0,1:T(8,128)} %fusion.39, f32[1280,1024]{1,0:T(8,128)} %copy-done.4, f32[576]{0:T(1024)S(1)} %slice.112, s32[640]{0:T(1024)S(1)} %add.143, s32[576]{0:T(1024)S(1)} %slice.111, pred[640]{0:T(1024)(128)(4,1)S(1)} %broadcast_compare_fusion), kind=kOutput, calls=%fused_computation.19 | convolution fusion | flops 2266767360 | bytes 7937664 | tf_op jit(solution)/shard_map/dot_general | solution.py:196
  453.0 1.7 copy.44
  (61 shorter events, 2.8 us)
Async XLA Ops:
  6.5 2.1 copy-start
  6.5 396.0 %all-gather.8.cloned.1.call-start = ((), (), s32[]{:S(2)}) async-start(), calls=%async_computation.2 | async-start | bytes 3891200 | tf_op jit(solution)/shard_map/all_gather | solution.py:144
  23.7 182.0 %copy-start.5 = (bf16[4,10,4,2432]{3,2,1,0:T(4,128)(2,1)}, bf16[4,10,4,2432]{3,2,1,0:T(4,128)(2,1)S(1)}, u32[]{:S(2)}) copy-start(bf16[4,10,4,2432]{3,2,1,0:T(4,128)(2,1)S(1)} %reshape.301) | copy-start | bytes 2334724
  205.7 4.9 %copy-start.8 = (f32[40]{0:T(128)S(1)}, f32[40]{0:T(128)}, u32[]{:S(2)}) copy-start(f32[40]{0:T(128)} %param.11) | copy-start | bytes 484
  208.9 200.0 %all-gather.6.cloned.1.call-start = ((), (), s32[]{:S(2)}) async-start(), calls=%async_computation.1 | async-start | bytes 3307520 | tf_op jit(solution)/shard_map/all_gather | solution.py:141
  400.6 1.9 copy-start.2
  415.0 6.8 %copy-start.6 = (bf16[640,2432]{1,0:T(8,128)(2,1)S(1)}, bf16[640,2432]{1,0:T(8,128)(2,1)}, u32[]{:S(2)}) copy-start(bf16[640,2432]{1,0:T(8,128)(2,1)} %reshape.304) | copy-start | bytes 9338884
  415.0 6.8 %copy-start.7 = (bf16[640,2432]{1,0:T(8,128)(2,1)S(1)}, bf16[640,2432]{1,0:T(8,128)(2,1)}, u32[]{:S(2)}) copy-start(bf16[640,2432]{1,0:T(8,128)(2,1)} %reshape.303) | copy-start | bytes 9338884
  421.8 10.5 %copy-start.3 = (f32[1024,1024]{1,0:T(8,128)S(1)}, f32[1024,1024]{1,0:T(8,128)}, u32[]{:S(2)}) copy-start(f32[1024,1024]{1,0:T(8,128)} %copy-done.2) | copy-start | bytes 12582916
  441.2 2.3 copy-start.4
  447.0 7.8 %copy-start.1 = (bf16[2,304,160]{1,2,0:T(8,128)(2,1)S(1)}, bf16[2,304,160]{1,2,0:T(8,128)(2,1)}, u32[]{:S(2)}) copy-start(bf16[2,304,160]{1,2,0:T(8,128)(2,1)} %param.8) | copy-start | bytes 583684
Sparse Core Ops, SparseCore 0:
  209.0 37.7 all-gather.7
  249.4 89.7 all-gather.5

commit v6 on v5

--- a/solution.py
+++ b/solution.py
@@ -11,6 +11,49 @@
 PANELS = 1
 NPAN = 10
 HI = lax.Precision.HIGHEST
+MESH = pl.DeviceIdType.MESH
+
+
+def _gather_kernel(x_ref, out_ref, local_sem, send_sem, recv_sem, *, axis, count):
+    me = lax.axis_index(axis)
+    barrier = pltpu.get_barrier_semaphore()
+    for step in range(1, count):
+        peer = lax.rem(me + step, count)
+        pl.semaphore_signal(barrier, inc=1, device_id={axis: peer}, device_id_type=MESH)
+    pl.semaphore_wait(barrier, count - 1)
+    own = pltpu.make_async_copy(x_ref, out_ref.at[me], local_sem)
+    own.start()
+    copies = []
+    for step in range(1, count):
+        peer = lax.rem(me + step, count)
+        copy = pltpu.make_async_remote_copy(
+            src_ref=x_ref,
+            dst_ref=out_ref.at[me],
+            send_sem=send_sem.at[step],
+            recv_sem=recv_sem.at[step],
+            device_id={axis: peer},
+            device_id_type=MESH,
+        )
+        copy.start()
+        copies.append(copy)
+    own.wait()
+    for copy in copies:
+        copy.wait()
+
+
+def remote_gather(x, axis, count, collective_id):
+    return pl.pallas_call(
+        functools.partial(_gather_kernel, axis=axis, count=count),
+        out_shape=jax.ShapeDtypeStruct((count,) + x.shape, x.dtype),
+        in_specs=[pl.BlockSpec(memory_space=pl.ANY)],
+        out_specs=pl.BlockSpec(memory_space=pl.ANY),
+        scratch_shapes=[
+            pltpu.SemaphoreType.DMA(()),
+            pltpu.SemaphoreType.DMA((count,)),
+            pltpu.SemaphoreType.DMA((count,)),
+        ],
+        compiler_params=pltpu.CompilerParams(collective_id=collective_id, has_side_effects=True),
+    )(x)
 
 
 def _base_inverse(s):
@@ -122,13 +165,8 @@
         split3(shift_grp[:, 0].reshape(-1))
     )
     panel_w = jnp.concatenate([every[:, 0].reshape(groups * window, total), panel_shift_row], 0)
-    panel_w = lax.all_to_all(
-        jnp.broadcast_to(panel_w[None], (rowcount * colcount,) + panel_w.shape),
-        ("row", "col"),
-        0,
-        0,
-        tiled=False,
-    ).reshape((rowcount, colcount) + panel_w.shape)
+    panel_w = remote_gather(panel_w, "col", colcount, 0)
+    panel_w = remote_gather(panel_w, "row", rowcount, 1)
     every, panel_w = lax.optimization_barrier((every, panel_w))
     shift_panel = join3(panel_w[:, :, groups * window, : 3 * groups * window])
     shift_panel = jnp.transpose(

time: 470 us -> 444 us (0.945)
  blocking collectives: 191 us -> 10.5 us
  Pallas kernels: 159 us -> 305 us
  local copies, waits for them, and re-layouts: 47.8 us -> 56.4 us
    all_to_all x1 -> x0, blocking collectives: 180 us -> none  [local(): lax.all_to_all(jnp.broadcast_to(panel_w[None], (rowcount * colcount,) + p...]
    pallas_call x0 -> x2, Pallas kernels: none -> 134 us  [remote_gather(): pl.pallas_call(functools.partial(_gather_kernel, axis=axis, count=count),...]
    reshape x0 -> x2, local copies, waits for them, and re-layouts: none -> 16.5 us  [local(): panel_w[:, :, :groups * window]]
    pallas_call x1, Pallas kernels: 159 us -> 171 us  [inverse_cholesky(): pl.pallas_call(functools.partial(_kernel, n=n, b=b), out_shape=jax.ShapeD...]
    transpose x1 -> x0, local copies, waits for them, and re-layouts: 6.15 us -> none  [local(): panel_w = jnp.transpose(panel_w, (2, 0, 1, 3, 4)).reshape(PW, total)]
  transfers between devices with their start and end apart: 2 -> 2, of which waited for: 0 -> 0; matrix products, arithmetic and copies ran while one was open for 8% -> 12% of each run, Pallas kernels for 34% -> 39%
where the time goes in v6:
time: 444 us; the launch traced here: 437 us
  Pallas kernels  305 us (69%)
  local copies, waits for them, and re-layouts  56.4 us (13%)
  matrix products  45.3 us (10%)
  between operations  13.9 us (3%)
  blocking collectives  10.5 us (2%)
  other arithmetic  5.62 us (1%)
    pallas_call x1, Pallas kernels, inverse_cholesky(): pl.pallas_call(functools.partial(_kernel, n=n, b=b), out_shape=jax.ShapeD...  171 us
    pallas_call x2, Pallas kernels, remote_gather(): pl.pallas_call(functools.partial(_gather_kernel, axis=axis, count=count),...  134 us
    reshape x2, local copies, waits for them, and re-layouts, local(): panel_w[:, :, :groups * window]  16.5 us
    dot_general x1, matrix products, local(): lax.dot_general(panel_w, panel_w, dims, preferred_element_type=f32)  10.9 us
    dot_general x1, matrix products, local(): lax.dot_general(both_w, panel_w, dims, preferred_element_type=f32)  10.7 us
    all_gather x1, blocking collectives, local(): lax.all_gather(jnp.concatenate([whitened, shift_row], axis=0), 'grp', axi...  10.5 us
    dot_general x1, matrix products, local(): lax.dot_general(both_panel, inverse_factor_panel, dims, precision=high, p...  8.88 us
  transfers between devices with their start and end apart: 2, of which 0 were waited for; matrix products, arithmetic and copies ran while one was open for 12% of the time, Pallas kernels for 39%

profile of v6, /device:TPU:1, one launch (start us, length us, event | category | flops | bytes accessed | tf_op | source)
XLA Modules:
  0.0 437.3 jit_solution(14162669990371028425)
XLA Ops:
  6.5 0.6 compare_reduce_fusion
  7.2 0.7 fusion.28
  7.8 0.7 compare_convert_fusion
  8.6 2.1 fusion.16
  11.1 0.7 broadcast_select_fusion.1
  11.8 10.5 %all-gather.2 = bf16[4,161,608]{2,1,0:T(8,128)(2,1)S(1)} all-gather(bf16[1,161,608]{2,1,0:T(8,128)(2,1)S(1)} %fusion.24), channel_id=2, replica_groups=mesh['grp'=4,'row'=4,'col'=16] {'grp'}, dimensions={0}, use_global_device_ids=true | all-gather | bytes 978880 | tf_op jit(solution)/shard_map/all_gather | solution.py:158
  22.9 0.8 reshape.297
  24.1 0.6 broadcast_select_fusion
  24.7 0.7 fusion.25.x_ref
  25.3 50.0 %shard_map.46.x_ref = bf16[16,17,2432]{2,1,0:T(8,128)(2,1)} custom-call(bf16[17,2432]{1,0:T(8,128)(2,1)} %fusion.25.x_ref), custom_call_target="tpu_custom_call" | custom-call | tf_op jit(solution)/shard_map/pallas_call | solution.py:45
  75.4 84.5 %shard_map.47 = bf16[4,16,17,2432]{3,2,1,0:T(8,128)(2,1)} custom-call(bf16[16,17,2432]{2,1,0:T(8,128)(2,1)} %shard_map.46.x_ref), custom_call_target="tpu_custom_call" | custom-call | tf_op jit(solution)/shard_map/pallas_call | solution.py:45
  159.9 1.7 constant_dynamic-slice_fusion.1
  162.6 4.9 %slice.91 = bf16[4,16,16,2432]{3,2,1,0:T(8,128)(2,1)} slice(bf16[4,16,17,2432]{3,2,1,0:T(8,128)(2,1)} %shard_map.47), slice={[0:4], [0:16], [0:16], [0:2432]} | slice | bytes 9961472 | tf_op jit(solution)/shard_map/slice | solution.py:175
  167.5 9.6 %reshape.300 = bf16[4,16,4,4,2432]{4,3,2,1,0:T(4,128)(2,1)} reshape(bf16[4,16,16,2432]{3,2,1,0:T(8,128)(2,1)} %slice.91) | data formatting | bytes 9961472 | tf_op jit(solution)/shard_map/reshape | solution.py:175
  177.1 6.9 %copy.35 = bf16[4,16,4,4,2432]{4,3,1,0,2:T(4,128)(2,1)} copy(bf16[4,16,4,4,2432]{4,3,2,1,0:T(4,128)(2,1)} %reshape.300) | data formatting | bytes 9961472 | tf_op jit(solution)/shard_map/reshape | solution.py:175
  184.0 8.7 %reshape.301 = bf16[1024,2432]{1,0:T(8,128)(2,1)} reshape(bf16[4,4,16,4,2432]{4,3,2,1,0:T(4,128)(2,1)} %bitcast.43) | data formatting | bytes 9961472 | tf_op jit(solution)/shard_map/reshape | solution.py:176
  192.7 1.0 convert_reduce_fusion
  194.3 10.9 %select_add_fusion.a_ref = f32[1024,1024]{1,0:T(8,128)} fusion(f32[1024]{0:T(1024)S(1)} %broadcast_in_dim.78, bf16[1024,2432]{1,0:T(8,128)(2,1)} %reshape.301), kind=kOutput, calls=%fused_computation.9 | convolution fusion | flops 5103419392 | bytes 9179136 | tf_op jit(solution)/shard_map/dot_general | solution.py:203
  205.2 171.0 %shard_map.48 = f32[1024,1024]{1,0:T(8,128)S(1)} custom-call(f32[1024,1024]{1,0:T(8,128)} %select_add_fusion.a_ref), custom_call_target="tpu_custom_call" | custom-call | flops 2147483648 | bytes 8388608 | tf_op jit(solution)/shard_map/pallas_call | solution.py:106
  376.1 1.9 copy-done.2
  378.1 3.1 copy.36
  381.2 3.0 reshape.299
  384.2 3.1 copy.26
  387.3 3.0 reshape.298
  390.3 6.8 %fusion.39 = f32[640,640]{0,1:T(8,128)} fusion(bf16[640,2432]{1,0:T(8,128)(2,1)} %reshape.298, bf16[640,2432]{1,0:T(8,128)(2,1)} %reshape.299), kind=kOutput, calls=%fused_computation.78 | convolution fusion | flops 1992294400 | bytes 7864320 | tf_op jit(solution)/shard_map/dot_general | solution.py:213
  397.2 10.7 %fusion = f32[1280,1024]{1,0:T(8,128)S(1)} fusion(bf16[1024,2432]{1,0:T(8,128)(2,1)} %reshape.301, bf16[640,2432]{1,0:T(8,128)(2,1)S(1)} %copy-done.6, bf16[640,2432]{1,0:T(8,128)(2,1)S(1)} %copy-done.7), kind=kOutput, calls=%fused_computation | convolution fusion | flops 6387793920 | bytes 16449536 | tf_op jit(solution)/shard_map/dot_general | solution.py:209
  407.9 8.9 %fusion.4 = f32[1280,1024]{1,0:T(8,128)S(1)} fusion(f32[1024,1024]{1,0:T(8,128)S(1)} %copy-done.3, f32[1280,1024]{1,0:T(8,128)S(1)} %fusion, f32[1024]{0:T(1024)S(1)} %broadcast_in_dim.78, s32[1280]{0:T(1024)S(1)} %pad_add_fusion), kind=kOutput, calls=%fused_computation.4 | convolution fusion | flops 8056995840 | bytes 14689280 | tf_op jit(solution)/shard_map/dot_general | solution.py:219
  416.8 2.3 copy-done.4
  419.2 2.1 copy.31
  421.3 1.0 constant_dynamic-slice_fusion
  422.5 5.9 %fusion.13 = f32[640,576]{0,1:T(8,128)S(1)} fusion(f32[640,640]{0,1:T(8,128)} %fusion.39, f32[1280,1024]{1,0:T(8,128)} %copy-done.4, f32[576]{0:T(1024)S(1)} %slice.112, s32[640]{0:T(1024)S(1)} %add.143, s32[576]{0:T(1024)S(1)} %slice.111, pred[640]{0:T(1024)(128)(4,1)S(1)} %broadcast_compare_fusion), kind=kOutput, calls=%fused_computation.20 | convolution fusion | flops 2266767360 | bytes 7937664 | tf_op jit(solution)/shard_map/dot_general | solution.py:234
  428.5 1.7 copy.32
  (61 shorter events, 3.2 us)
Async XLA Ops:
  6.5 2.0 copy-start
  6.5 371.5 %all-gather.8.cloned.1.call-start = ((), (), s32[]{:S(2)}) async-start(), calls=%async_computation.1 | async-start | bytes 3891200 | tf_op jit(solution)/shard_map/all_gather | solution.py:182
  23.7 136.2 %copy-start.5 = (bf16[4,10,4,2432]{3,2,1,0:T(4,128)(2,1)}, bf16[4,10,4,2432]{3,2,1,0:T(4,128)(2,1)S(1)}, u32[]{:S(2)}) copy-start(bf16[4,10,4,2432]{3,2,1,0:T(4,128)(2,1)S(1)} %reshape.297) | copy-start | bytes 2334724
  75.4 86.3 %copy-start.8 = (f32[40]{0:T(128)S(1)}, f32[40]{0:T(128)}, u32[]{:S(2)}) copy-start(f32[40]{0:T(128)} %param.11) | copy-start | bytes 484
  159.9 224.3 %all-gather.6.cloned.1.call-start = ((), (), s32[]{:S(2)}) async-start(), calls=%async_computation | async-start | bytes 3307520 | tf_op jit(solution)/shard_map/all_gather | solution.py:179
  376.1 1.9 copy-start.2
  390.3 6.8 %copy-start.6 = (bf16[640,2432]{1,0:T(8,128)(2,1)S(1)}, bf16[640,2432]{1,0:T(8,128)(2,1)}, u32[]{:S(2)}) copy-start(bf16[640,2432]{1,0:T(8,128)(2,1)} %reshape.299) | copy-start | bytes 9338884
  390.3 6.8 %copy-start.7 = (bf16[640,2432]{1,0:T(8,128)(2,1)S(1)}, bf16[640,2432]{1,0:T(8,128)(2,1)}, u32[]{:S(2)}) copy-start(bf16[640,2432]{1,0:T(8,128)(2,1)} %reshape.298) | copy-start | bytes 9338884
  397.2 10.7 %copy-start.3 = (f32[1024,1024]{1,0:T(8,128)S(1)}, f32[1024,1024]{1,0:T(8,128)}, u32[]{:S(2)}) copy-start(f32[1024,1024]{1,0:T(8,128)} %copy-done.2) | copy-start | bytes 12582916
  416.7 2.3 copy-start.4
  422.5 7.8 %copy-start.1 = (bf16[2,304,160]{1,2,0:T(8,128)(2,1)S(1)}, bf16[2,304,160]{1,2,0:T(8,128)(2,1)}, u32[]{:S(2)}) copy-start(bf16[2,304,160]{1,2,0:T(8,128)(2,1)} %param.8) | copy-start | bytes 583684
Sparse Core Ops, SparseCore 0:
  160.0 42.4 all-gather.7
  205.1 89.8 all-gather.5
